TPU v7x, 32 devices: a whole 2x2x4 slice. The times are simulated.
32 devices in a mesh: dp: 8 (over z, x), tensor: 4 (over y, core).
Axes of the slice: x: 2, y: 2, z: 4, core: 2. Of those that a mesh axis runs over, the one named last changes fastest.
Arguments:
- tokens: bfloat16 [32768, 768], P(('dp', 'tensor')), may hold values from -6 to 6
- segment_ids: int32 [16, 2048], P('dp'), may hold values from 0 to 8, as said below
- memory_positions: int32 [16, 20], P('dp'), may hold values from 0 to 2047, as said below
- memory_rows: bfloat16 [20, 768], replicated, may hold values from -6 to 6
- qkv_weight: bfloat16 [768, 12, 192], P('dp', 'tensor'), may hold values from -0.21875 to 0.21875
- qv_bias: bfloat16 [12, 128], P('tensor'), may hold values from -3 to 3
- out_weight: bfloat16 [768, 12, 64], P('dp', 'tensor'), may hold values from -0.875 to 0.875
- out_bias: bfloat16 [768], replicated, may hold values from -1.75 to 1.75
- norm1_gain: bfloat16 [768], replicated, may hold values from 0.5 to 1.5
- norm1_bias: bfloat16 [768], replicated, may hold values from -1.75 to 1.75
- up_weight: bfloat16 [768, 3072], P('dp', 'tensor'), may hold values from -0.21875 to 0.21875
- up_bias: bfloat16 [3072], P('tensor'), may hold values from -3 to 3
- down_weight: bfloat16 [768, 3072], P('dp', 'tensor'), may hold values from -0.109375 to 0.109375
- down_bias: bfloat16 [768], replicated, may hold values from -1.75 to 1.75
- norm2_gain: bfloat16 [768], replicated, may hold values from 0.5 to 1.5
- norm2_bias: bfloat16 [768], replicated, may hold values from -1.75 to 1.75
- out_cotangent: bfloat16 [32768, 768], P(('dp', 'tensor')), may hold values from -6 to 6
Outputs:
- block_out: bfloat16 [32768, 768], P(('dp', 'tensor'))
- grad_tokens: float32 [32768, 768], P(('dp', 'tensor'))
- grad_memory_rows: float32 [20, 768], replicated
- grad_qkv_weight: float32 [768, 12, 192], P('dp', 'tensor')
- grad_qv_bias: float32 [12, 128], P('tensor')
- grad_out_weight: float32 [768, 12, 64], P('dp', 'tensor')
- grad_out_bias: float32 [768], replicated
- grad_norm1_gain: float32 [768], replicated
- grad_norm1_bias: float32 [768], replicated
- grad_up_weight: float32 [768, 3072], P('dp', 'tensor')
- grad_up_bias: float32 [3072], P('tensor')
- grad_down_weight: float32 [768, 3072], P('dp', 'tensor')
- grad_down_bias: float32 [768], replicated
- grad_norm2_gain: float32 [768], replicated
- grad_norm2_bias: float32 [768], replicated
Inputs may be any that keep to these rules, and one draw needn't show every extreme that they name: `segment_ids`: never falling along a group; each group begins with segment 0 of at least 512 positions and holds every segment up to 8. `memory_positions`: within a group all positions differ; read rows lie among the first 512 positions, the first at 0, write rows among the last 512, the first at 2047.
All inputs are finite; a program needn't handle non-finite values.
Results may differ from a plain program's by a relative error of at most 0.015.
Values may be sent and summed in bfloat16 or wider, within the bound.
A program may use at most 192 MiB of HBM per device.

v0:
```python
import jax
import jax.numpy as jnp
from jax import lax
from jax.sharding import PartitionSpec as P

QBLOCK = 512


EPSILON = 1e-12
MASKED = -1e30


def layer_norm(values, norm_gain, norm_shift):
    centre = values - jnp.mean(values, axis=-1, keepdims=True)
    spread = jnp.mean(centre * centre, axis=-1, keepdims=True)
    return centre * lax.rsqrt(spread + EPSILON) * norm_gain + norm_shift


def gelu_exact(values):
    return jax.nn.gelu(values, approximate=False)


def block_inputs(block_index, segments, query_all, key_all, value_all, score_scale):
    group_len = segments.shape[1]
    block_count = group_len // QBLOCK
    group_index = block_index // block_count
    within = block_index % block_count * QBLOCK
    first_row = group_index * group_len + within
    query_rows = lax.dynamic_slice_in_dim(query_all, first_row, QBLOCK, 0)
    key_rows = lax.dynamic_slice_in_dim(key_all, group_index * group_len, group_len, 0)
    value_rows = lax.dynamic_slice_in_dim(value_all, group_index * group_len, group_len, 0)
    group_segments = lax.dynamic_index_in_dim(segments, group_index, 0, keepdims=False)
    query_segments = lax.dynamic_slice_in_dim(group_segments, within, QBLOCK, 0)
    visible = (group_segments[None, :] == 0) | (group_segments[None, :] == query_segments[:, None])
    scores = (
        jnp.einsum("bhe,ghe->hbg", query_rows, key_rows, preferred_element_type=jnp.float32)
        * score_scale
    )
    scores = jnp.where(visible[None], scores, MASKED)
    return (first_row, group_index * group_len, query_rows, key_rows, value_rows, scores)


def attend_forward(query_all, key_all, value_all, segments, score_scale):
    block_total = query_all.shape[0] // QBLOCK

    def one_block(block_index):
        _, _, _, _, value_rows, scores = block_inputs(
            block_index, segments, query_all, key_all, value_all, score_scale
        )
        row_peak = jnp.max(scores, axis=-1, keepdims=True)
        exp_scores = jnp.exp(scores - row_peak)
        row_total = jnp.sum(exp_scores, axis=-1, keepdims=True)
        weights = (exp_scores / row_total).astype(jnp.bfloat16)
        head_mixed = jnp.einsum(
            "hbg,ghe->bhe", weights, value_rows, preferred_element_type=jnp.float32
        )
        return (head_mixed.astype(jnp.bfloat16), (row_peak + jnp.log(row_total))[..., 0])

    head_mixed, log_totals = lax.map(one_block, jnp.arange(block_total, dtype=jnp.int32))
    return (head_mixed.reshape(query_all.shape), log_totals)


def attend_backward(query_all, key_all, value_all, grad_mixed, log_totals, segments, score_scale):
    group_len = segments.shape[1]
    block_total = query_all.shape[0] // QBLOCK

    def one_block(block_index, grads):
        grad_query, grad_key, grad_value = grads
        first_row, key_start, query_rows, key_rows, value_rows, scores = block_inputs(
            block_index, segments, query_all, key_all, value_all, score_scale
        )
        weights = jnp.exp(scores - log_totals[block_index][..., None])
        grad_rows = lax.dynamic_slice_in_dim(grad_mixed, first_row, QBLOCK, 0)
        grad_weights = jnp.einsum(
            "bhe,ghe->hbg", grad_rows, value_rows, preferred_element_type=jnp.float32
        )
        grad_scores = weights * (
            grad_weights - jnp.sum(weights * grad_weights, axis=-1, keepdims=True)
        )
        grad_scores = grad_scores.astype(jnp.bfloat16)
        part_query = (
            jnp.einsum("hbg,ghe->bhe", grad_scores, key_rows, preferred_element_type=jnp.float32)
            * score_scale
        )
        part_key = (
            jnp.einsum("hbg,bhe->ghe", grad_scores, query_rows, preferred_element_type=jnp.float32)
            * score_scale
        )
        part_value = jnp.einsum(
            "hbg,bhe->ghe",
            weights.astype(jnp.bfloat16),
            grad_rows,
            preferred_element_type=jnp.float32,
        )
        grad_query = lax.dynamic_update_slice_in_dim(grad_query, part_query, first_row, 0)
        old_key = lax.dynamic_slice_in_dim(grad_key, key_start, group_len, 0)
        grad_key = lax.dynamic_update_slice_in_dim(grad_key, old_key + part_key, key_start, 0)
        old_value = lax.dynamic_slice_in_dim(grad_value, key_start, group_len, 0)
        grad_value = lax.dynamic_update_slice_in_dim(
            grad_value, old_value + part_value, key_start, 0
        )
        return (grad_query, grad_key, grad_value)

    zero_rows = jnp.zeros(query_all.shape, jnp.float32)
    return lax.fori_loop(0, block_total, one_block, (zero_rows, zero_rows, zero_rows))


def shards(
    tokens,
    segment_ids,
    memory_positions,
    memory_rows,
    qkv_weight,
    qv_bias,
    out_weight,
    out_bias,
    norm1_gain,
    norm1_bias,
    up_weight,
    up_bias,
    down_weight,
    down_bias,
    norm2_gain,
    norm2_bias,
    out_cotangent,
):
    row_count, model_width = tokens.shape
    group_count, group_len = segment_ids.shape
    head_dim = out_weight.shape[2]
    score_scale = float(head_dim) ** (-0.5)
    row_place = lax.axis_index("tensor") * row_count + jnp.arange(row_count, dtype=jnp.int32)
    targets = (
        memory_positions + group_len * jnp.arange(group_count, dtype=jnp.int32)[:, None]
    ).reshape(-1)
    memory_picks = (row_place[:, None] == targets[None, :]).astype(jnp.float32)
    memory_table = jnp.tile(memory_rows.astype(jnp.float32), (group_count, 1))
    inputs = tokens.astype(jnp.float32) + jnp.dot(
        memory_picks, memory_table, precision=lax.Precision.HIGHEST
    )
    w_qkv, w_out, w_up, w_down = (
        lax.all_gather(qkv_weight, "dp", axis=0, tiled=True),
        lax.all_gather(out_weight, "dp", axis=0, tiled=True),
        lax.all_gather(up_weight, "dp", axis=0, tiled=True),
        lax.all_gather(down_weight, "dp", axis=0, tiled=True),
    )
    gain_one = norm1_gain.astype(jnp.float32)
    shift_one = norm1_bias.astype(jnp.float32)
    gain_two = norm2_gain.astype(jnp.float32)
    shift_two = norm2_bias.astype(jnp.float32)
    inputs_low = inputs.astype(jnp.bfloat16)
    all_inputs = lax.all_gather(inputs_low, "tensor", axis=0, tiled=True)
    bias_query = qv_bias[:, :head_dim].astype(jnp.float32)
    bias_value = qv_bias[:, head_dim:].astype(jnp.float32)
    qkv_bias = jnp.concatenate([bias_query, jnp.zeros_like(bias_query), bias_value], axis=-1)
    projected = (
        jnp.einsum("td,dhe->the", all_inputs, w_qkv, preferred_element_type=jnp.float32) + qkv_bias
    )
    projected = projected.astype(jnp.bfloat16)
    query_all = projected[..., :head_dim]
    key_all = projected[..., head_dim : 2 * head_dim]
    value_all = projected[..., 2 * head_dim :]
    head_mixed, log_totals = attend_forward(query_all, key_all, value_all, segment_ids, score_scale)
    row_piece = head_mixed
    attended = lax.psum_scatter(
        jnp.einsum("the,dhe->td", row_piece, w_out, preferred_element_type=jnp.float32),
        "tensor",
        scatter_dimension=0,
        tiled=True,
    ) + out_bias.astype(jnp.float32)
    first_sum = inputs + attended
    hidden = layer_norm(first_sum, gain_one, shift_one)
    hidden_low = hidden.astype(jnp.bfloat16)
    all_hidden = lax.all_gather(hidden_low, "tensor", axis=0, tiled=True)
    pre_act = jnp.dot(all_hidden, w_up, preferred_element_type=jnp.float32) + up_bias.astype(
        jnp.float32
    )
    activated = gelu_exact(pre_act).astype(jnp.bfloat16)
    row_piece = activated
    branch = lax.psum_scatter(
        jnp.einsum("tf,df->td", row_piece, w_down, preferred_element_type=jnp.float32),
        "tensor",
        scatter_dimension=0,
        tiled=True,
    )
    second_sum = hidden + branch + down_bias.astype(jnp.float32)
    block_out = layer_norm(second_sum, gain_two, shift_two).astype(jnp.bfloat16)
    cotangent = out_cotangent.astype(jnp.float32)
    _, norm_two_back = jax.vjp(layer_norm, second_sum, gain_two, shift_two)
    grad_second, grad_gain_two, grad_shift_two = norm_two_back(cotangent)
    grad_branch_low = grad_second.astype(jnp.bfloat16)
    grad_down_bias = jnp.sum(grad_branch_low.astype(jnp.float32), axis=0)
    all_grad_branch = lax.all_gather(grad_branch_low, "tensor", axis=0, tiled=True)
    grad_act = jnp.einsum("td,df->tf", all_grad_branch, w_down, preferred_element_type=jnp.float32)
    grad_down = jnp.einsum(
        "td,tf->df", all_grad_branch, activated, preferred_element_type=jnp.float32
    )
    grad_pre = jax.vjp(gelu_exact, pre_act)[1](grad_act)[0].astype(jnp.bfloat16)
    grad_up = jnp.einsum("td,tf->df", all_hidden, grad_pre, preferred_element_type=jnp.float32)
    grad_up_bias = jnp.sum(grad_pre.astype(jnp.float32), axis=0)
    row_piece = grad_pre
    grad_hidden = (
        lax.psum_scatter(
            jnp.einsum("tf,df->td", row_piece, w_up, preferred_element_type=jnp.float32),
            "tensor",
            scatter_dimension=0,
            tiled=True,
        )
        + grad_second
    )
    _, norm_one_back = jax.vjp(layer_norm, first_sum, gain_one, shift_one)
    grad_first, grad_gain_one, grad_shift_one = norm_one_back(grad_hidden)
    grad_attended_low = grad_first.astype(jnp.bfloat16)
    grad_out_bias = jnp.sum(grad_attended_low.astype(jnp.float32), axis=0)
    all_grad_attended = lax.all_gather(grad_attended_low, "tensor", axis=0, tiled=True)
    grad_mixed = jnp.einsum(
        "td,dhe->the", all_grad_attended, w_out, preferred_element_type=jnp.float32
    ).astype(jnp.bfloat16)
    grad_out = jnp.einsum(
        "td,the->dhe", all_grad_attended, head_mixed, preferred_element_type=jnp.float32
    )
    grad_query, grad_key, grad_value = attend_backward(
        query_all, key_all, value_all, grad_mixed, log_totals, segment_ids, score_scale
    )
    grad_projected = jnp.concatenate([grad_query, grad_key, grad_value], axis=-1).astype(
        jnp.bfloat16
    )
    grad_qkv = jnp.einsum(
        "td,the->dhe", all_inputs, grad_projected, preferred_element_type=jnp.float32
    )
    bias_sums = jnp.sum(grad_projected.astype(jnp.float32), axis=0)
    grad_qv_bias = jnp.concatenate([bias_sums[:, :head_dim], bias_sums[:, 2 * head_dim :]], axis=-1)
    row_piece = grad_projected
    grad_tokens = (
        lax.psum_scatter(
            jnp.einsum("the,dhe->td", row_piece, w_qkv, preferred_element_type=jnp.float32).astype(
                jnp.bfloat16
            ),
            "tensor",
            scatter_dimension=0,
            tiled=True,
        ).astype(jnp.float32)
        + grad_first
    )
    grad_memory = jnp.dot(memory_picks.T, grad_tokens, precision=lax.Precision.HIGHEST)
    grad_memory = jnp.sum(grad_memory.reshape(group_count, -1, model_width), axis=0)
    grad_qkv, grad_out, grad_up, grad_down = (
        lax.psum_scatter(grad_qkv, "dp", scatter_dimension=0, tiled=True),
        lax.psum_scatter(grad_out, "dp", scatter_dimension=0, tiled=True),
        lax.psum_scatter(grad_up, "dp", scatter_dimension=0, tiled=True),
        lax.psum_scatter(grad_down, "dp", scatter_dimension=0, tiled=True),
    )
    grad_qv_bias, grad_up_bias = lax.psum((grad_qv_bias, grad_up_bias), "dp")
    (
        grad_memory,
        grad_out_bias,
        grad_gain_one,
        grad_shift_one,
        grad_down_bias,
        grad_gain_two,
        grad_shift_two,
    ) = lax.psum(
        (
            grad_memory,
            grad_out_bias,
            grad_gain_one,
            grad_shift_one,
            grad_down_bias,
            grad_gain_two,
            grad_shift_two,
        ),
        ("dp", "tensor"),
    )
    return (
        block_out,
        grad_tokens,
        grad_memory,
        grad_qkv,
        grad_qv_bias,
        grad_out,
        grad_out_bias,
        grad_gain_one,
        grad_shift_one,
        grad_up,
        grad_up_bias,
        grad_down,
        grad_down_bias,
        grad_gain_two,
        grad_shift_two,
    )


def solution(mesh):
    in_specs = (
        P(("dp", "tensor"), None),
        P("dp", None),
        P("dp", None),
        P(),
        P("dp", "tensor", None),
        P("tensor", None),
        P("dp", "tensor", None),
        P(),
        P(),
        P(),
        P("dp", "tensor"),
        P("tensor"),
        P("dp", "tensor"),
        P(),
        P(),
        P(),
        P(("dp", "tensor"), None),
    )
    out_specs = (
        P(("dp", "tensor"), None),
        P(("dp", "tensor"), None),
        P(),
        P("dp", "tensor", None),
        P("tensor", None),
        P("dp", "tensor", None),
        P(),
        P(),
        P(),
        P("dp", "tensor"),
        P("tensor"),
        P("dp", "tensor"),
        P(),
        P(),
        P(),
    )
    return jax.shard_map(shards, mesh=mesh, in_specs=in_specs, out_specs=out_specs, check_vma=False)
```

profile of v0, /device:TPU:0, one launch (start us, length us, event | category | flops | bytes accessed | tf_op | source)
XLA Modules:
  0.0 1528.1 jit_solution(10689661794506984223)
XLA Ops:
  15.6 39.0 %all_gather.25 = bf16[768,3,192]{2,1,0:T(4,128)(2,1)S(1)} all-gather(bf16[96,3,192]{2,1,0:T(4,128)(2,1)S(1)} %copy.60), channel_id=1, replica_groups=mesh['dp'=8,'tensor'=4] {'dp'}, dimensions={0}, use_global_device_ids=true | all-gather | bytes 995328 | tf_op jit(solution)/shard_map/all_gather | solution.py:141
  55.6 32.3 %all_gather.26 = bf16[768,3,64]{2,1,0:T(4,128)(2,1)S(1)} all-gather(bf16[96,3,64]{2,1,0:T(4,128)(2,1)S(1)} %copy.64), channel_id=1, replica_groups=mesh['dp'=8,'tensor'=4] {'dp'}, dimensions={0}, use_global_device_ids=true | all-gather | bytes 331776 | tf_op jit(solution)/shard_map/all_gather | solution.py:142
  98.0 205.0 %while.35 = (s32[]{:T(128)}, bf16[8,512,3,64]{1,3,2,0:T(8,128)(2,1)}, f32[8,3,512]{2,1,0:T(4,128)}, s32[8]{0:T(128)S(1)}, bf16[4096,3,64]{0,2,1:T(8,128)(2,1)}, ...) while((s32[]{:T(128)}, ...), condition=%wide.region_3.4_spmd, body=%wide.region_0.3_spmd.sunk | while | flops 845251072 | bytes 50292328 | solution.py:59
  116.3 7.3 fusion.129
  141.9 7.3 fusion.129
  167.6 7.3 fusion.129
  193.2 7.3 fusion.129
  218.8 7.3 fusion.129
  244.4 7.3 fusion.129
  270.1 7.3 fusion.129
  295.7 7.3 fusion.129
  312.8 95.4 %reduce-scatter.11.cloned.1.call-done = f32[1024,768]{0,1:T(8,128)} async-done(((f32[4096,768]{0,1:T(8,128)}), f32[1024,768]{0,1:T(8,128)}) %reduce-scatter.11.cloned.1.call-update) | async-done | bytes 3145744 | tf_op jit(solution)/shard_map/reduce_scatter | solution.py:164
  414.9 45.6 %all-gather.9.cloned.1.call-done = bf16[4096,768]{0,1:T(8,128)(2,1)} async-done(((bf16[1024,768]{0,1:T(8,128)(2,1)}), bf16[4096,768]{0,1:T(8,128)(2,1)}) %all-gather.9.cloned.1.call-update) | async-done | bytes 6291472 | tf_op jit(solution)/shard_map/all_gather | solution.py:173
  460.5 35.6 %multiply_convert_fusion.1 = (bf16[4096,768]{1,0:T(8,128)(2,1)}, f32[4096,768]{1,0:T(8,128)}, f32[4096,768]{1,0:T(8,128)}) fusion(f32[768]{0:T(1024)S(1)} %convert_element_type.132, bf16[4096,768]{0,1:T(8,128)(2,1)} %all-gather.9.cloned.1.call-done, bf16[768,768]{1,0:T(8,128)(2,1)} %all-gather.11.cloned.1.call-done), kind=kOutput, calls=%fused_computation.62 | convolution fusion | flops 5039456256 | bytes 38931456 | tf_op jit(solution)/shard_map/dot_general | solution.py:174
  496.1 7.9 all-gather.13.cloned.1.call-done
  504.0 10.1 fusion.78
  517.4 92.3 %reduce-scatter.13.cloned.1.call-done = f32[1024,768]{0,1:T(8,128)} async-done(((f32[4096,768]{0,1:T(8,128)}), f32[1024,768]{0,1:T(8,128)}) %reduce-scatter.13.cloned.1.call-update) | async-done | bytes 3145744 | tf_op jit(solution)/shard_map/reduce_scatter | solution.py:179
  619.6 46.3 %all-gather.15.cloned.1.call-done = bf16[4096,768]{0,1:T(8,128)(2,1)} async-done(((bf16[1024,768]{0,1:T(8,128)(2,1)}), bf16[4096,768]{0,1:T(8,128)(2,1)}) %all-gather.15.cloned.1.call-update) | async-done | bytes 6291472 | tf_op jit(solution)/shard_map/all_gather | solution.py:192
  665.9 19.8 %convert_reduce_fusion = (f32[768]{0:T(1024)}, bf16[4096,768]{1,0:T(8,128)(2,1)}) fusion(f32[4096,768]{1,0:T(8,128)} %get-tuple-element.552, f32[4096,768]{1,0:T(8,128)} %get-tuple-element.571, f32[768]{0:T(1024)S(1)} %convert_element_type.132, bf16[4096,768]{0,1:T(8,128)(2,1)} %all-gather.15.cloned.1.call-done, ...), kind=kOutput, calls=%fused_computation.60 | convolution fusion | flops 4885314560 | bytes 38934528 | tf_op jit(solution)/shard_map/td,df->tf/dot_general | solution.py:193
  685.7 10.7 fusion.79
  697.0 96.5 %reduce-scatter.15.cloned.1.call-done = f32[1024,768]{0,1:T(8,128)} async-done(((f32[4096,768]{0,1:T(8,128)}), f32[1024,768]{0,1:T(8,128)}) %reduce-scatter.15.cloned.1.call-update) | async-done | bytes 3145744 | tf_op jit(solution)/shard_map/reduce_scatter | solution.py:202
  805.9 45.1 %all-gather.17.cloned.1.call-done = bf16[4096,768]{0,1:T(8,128)(2,1)} async-done(((bf16[1024,768]{0,1:T(8,128)(2,1)}), bf16[4096,768]{0,1:T(8,128)(2,1)}) %all-gather.17.cloned.1.call-update) | async-done | bytes 6291472 | tf_op jit(solution)/shard_map/all_gather | solution.py:214
  860.7 294.6 %while.36 = (s32[]{:T(128)}, bf16[4096,3,64]{0,2,1:T(8,128)(2,1)}, f32[4096,3,64]{0,2,1:T(8,128)}, f32[4096,3,64]{0,2,1:T(8,128)}, bf16[4096,3,64]{0,2,1:T(8,128...) while((s32[]{:T(128)}, bf16[4096,3,64]{0,2,1:T(8,128)(2,1)}, ...), condition=%wide.region_17.18_spmd, body=%wide.region_15.17_spmd.sunk | while | flops 2063827456 | bytes 181875408 | solution.py:105
  860.9 7.3 fusion.138
  870.7 7.9 multiply_reduce_fusion.6
  897.6 7.3 fusion.138
  907.5 7.9 multiply_reduce_fusion.6
  934.4 7.3 fusion.138
  944.2 7.9 multiply_reduce_fusion.6
  971.2 7.3 fusion.138
  981.0 7.9 multiply_reduce_fusion.6
  1007.9 7.3 fusion.138
  1017.7 7.9 multiply_reduce_fusion.6
  1044.7 7.3 fusion.138
  1054.5 7.9 multiply_reduce_fusion.6
  1081.4 7.3 fusion.138
  1091.3 7.9 multiply_reduce_fusion.6
  1118.2 7.3 fusion.138
  1128.0 7.9 multiply_reduce_fusion.6
  1177.3 11.4 fusion.82
  1188.8 10.6 fusion.81
  1199.6 9.8 fusion.54
  1215.0 11.4 reduce-scatter.17.cloned.1.call-done
  1232.7 22.2 %all-reduce.1 = (f32[3,128]{1,0:T(4,128)}, f32[768]{0:T(1024)}) all-reduce(f32[3,128]{1,0:T(4,128)S(1)} %pad_maximum_fusion.2, f32[768]{0:T(1024)S(1)} %copy-done.31), channel_id=1, replica_groups=mesh['dp'=8,'tensor'=4] {'dp'}, use_global_device_ids=true, to_apply=%region_23.24 | all-reduce | flops 1152 | bytes 9216 | tf_op jit(solution)/shard_map/psum | solution.py:252
  1254.9 37.9 %reduce-scatter.25.cloned.1.call-done = f32[96,192]{1,0:T(8,128)} async-done(((f32[768,192]{1,0:T(8,128)}), f32[96,192]{1,0:T(8,128)}) %reduce-scatter.25.cloned.1.call-update) | async-done | bytes 73744
  1298.0 67.8 %reduce-scatter.23.cloned.1.call-done = f32[96,768]{1,0:T(8,128)} async-done(((f32[768,768]{1,0:T(8,128)}), f32[96,768]{1,0:T(8,128)}) %reduce-scatter.23.cloned.1.call-update) | async-done | bytes 294928 | tf_op jit(solution)/shard_map/reduce_scatter | solution.py:250
  1365.8 72.8 %reduce-scatter.21.cloned.1.call-done = f32[96,768]{1,0:T(8,128)} async-done(((f32[768,768]{1,0:T(8,128)}), f32[96,768]{1,0:T(8,128)}) %reduce-scatter.21.cloned.1.call-update) | async-done | bytes 294928 | tf_op jit(solution)/shard_map/reduce_scatter | solution.py:249
  1438.6 73.0 %reduce-scatter.19.cloned.1.call-done = f32[96,3,192]{2,0,1:T(8,128)} async-done(((f32[768,3,192]{2,0,1:T(8,128)}), f32[96,3,192]{2,0,1:T(8,128)}) %reduce-scatter.19.cloned.1.call-update) | async-done | bytes 221200 | tf_op jit(solution)/shard_map/reduce_scatter | solution.py:247
  (440 shorter events, 415.6 us)
Async XLA Ops:
  8.0 80.6 %all-gather.7.cloned.1.call-start = ((), (), s32[]{:S(2)}) async-start(), calls=%async_computation.8 | async-start | bytes 7864320 | tf_op jit(solution)/shard_map/all_gather | solution.py:151
  15.4 40.1 %copy-start.23 = (bf16[96,3,64]{0,2,1:T(8,128)(2,1)S(1)}, bf16[96,3,64]{0,2,1:T(8,128)(2,1)}, u32[]{:S(2)}) copy-start(bf16[96,3,64]{0,2,1:T(8,128)(2,1)} %param.27) | copy-start | bytes 110596
  15.4 73.2 %copy-start.30 = (bf16[3,128]{1,0:T(4,128)(2,1)S(1)}, bf16[3,128]{1,0:T(4,128)(2,1)}, u32[]{:S(2)}) copy-start(bf16[3,128]{1,0:T(4,128)(2,1)} %param.26) | copy-start | bytes 2308
  15.4 392.8 %reduce-scatter.11.cloned.1.call-start = ((), (), s32[]{:S(2)}) async-start(), calls=%async_computation.9 | async-start | bytes 15728640 | tf_op jit(solution)/shard_map/reduce_scatter | solution.py:164
  55.5 39.1 %copy-start.18 = (bf16[768,3,192]{0,2,1:T(8,128)(2,1)}, bf16[768,3,192]{0,2,1:T(8,128)(2,1)S(1)}, u32[]{:S(2)}) copy-start(bf16[768,3,192]{0,2,1:T(8,128)(2,1)S(1)} %copy.62) | copy-start | bytes 2654212
  88.4 216.7 %copy-start.16 = (bf16[768,3,64]{0,2,1:T(8,128)(2,1)}, bf16[768,3,64]{0,2,1:T(8,128)(2,1)S(1)}, u32[]{:S(2)}) copy-start(bf16[768,3,64]{0,2,1:T(8,128)(2,1)S(1)} %copy.65) | copy-start | bytes 884740
  303.0 8.5 copy-start.4
  311.6 103.3 %all-gather.11.cloned.1.call-start = ((), (), s32[]{:S(2)}) async-start(), calls=%async_computation.11 | async-start | bytes 1327104 | tf_op jit(solution)/shard_map/all_gather | solution.py:143
  312.2 148.3 %all-gather.9.cloned.1.call-start = ((), (), s32[]{:S(2)}) async-start(), calls=%async_computation.10 | async-start | bytes 7864320 | tf_op jit(solution)/shard_map/all_gather | solution.py:173
  412.5 83.6 %copy-start.26 = (f32[1024]{0:T(1024)}, f32[1024]{0:T(1024)S(1)}, u32[]{:S(2)}) copy-start(f32[1024]{0:T(1024)S(1)} %multiply_reduce_fusion.4) | copy-start | bytes 12292
  414.2 89.8 %all-gather.13.cloned.1.call-start = ((), (), s32[]{:S(2)}) async-start(), calls=%async_computation.12 | async-start | bytes 1327104 | tf_op jit(solution)/shard_map/all_gather | solution.py:144
  414.7 195.0 %reduce-scatter.13.cloned.1.call-start = ((), (), s32[]{:S(2)}) async-start(), calls=%async_computation.13 | async-start | bytes 15728640 | tf_op jit(solution)/shard_map/reduce_scatter | solution.py:179
  514.2 151.7 %all-gather.15.cloned.1.call-start = ((), (), s32[]{:S(2)}) async-start(), calls=%async_computation.14 | async-start | bytes 7864320 | tf_op jit(solution)/shard_map/all_gather | solution.py:192
  619.4 174.2 %reduce-scatter.15.cloned.1.call-start = ((), (), s32[]{:S(2)}) async-start(), calls=%async_computation.15 | async-start | bytes 15728640 | tf_op jit(solution)/shard_map/reduce_scatter | solution.py:202
  665.9 19.8 %copy-start.41 = (bf16[768,768]{1,0:T(8,128)(2,1)S(1)}, bf16[768,768]{1,0:T(8,128)(2,1)}, u32[]{:S(2)}) copy-start(bf16[768,768]{1,0:T(8,128)(2,1)} %all-gather.11.cloned.1.call-done) | copy-start | bytes 3538948
  696.4 154.7 %all-gather.17.cloned.1.call-start = ((), (), s32[]{:S(2)}) async-start(), calls=%async_computation.16 | async-start | bytes 7864320 | tf_op jit(solution)/shard_map/all_gather | solution.py:214
  697.0 102.9 %copy-start.27 = (f32[1024]{0:T(1024)S(1)}, f32[1024]{0:T(1024)}, u32[]{:S(2)}) copy-start(f32[1024]{0:T(1024)} %copy-done.26) | copy-start | bytes 12292
  800.9 50.2 %copy-start.17 = (bf16[768,3,64]{0,2,1:T(8,128)(2,1)S(1)}, bf16[768,3,64]{0,2,1:T(8,128)(2,1)}, u32[]{:S(2)}) copy-start(bf16[768,3,64]{0,2,1:T(8,128)(2,1)} %copy-done.16) | copy-start | bytes 884740
  804.5 421.9 %reduce-scatter.17.cloned.1.call-start = ((), (), s32[]{:S(2)}) async-start(), calls=%async_computation.17 | async-start | bytes 7864320 | tf_op jit(solution)/shard_map/reduce_scatter | solution.py:234
  870.7 7.9 slice-start.1
  870.7 8.9 slice-start.2
  907.5 7.9 slice-start
  907.5 7.9 slice-start.1
  907.5 8.9 slice-start.2
  944.2 8.9 slice-start.2
  981.0 7.9 slice-start.1
  981.0 8.9 slice-start.2
  1017.7 7.9 slice-start.1
  1017.7 8.9 slice-start.2
  1054.5 7.9 slice-start.1
  1054.5 8.9 slice-start.2
  1091.3 7.9 slice-start
  1091.3 8.0 slice-start.1
  1091.3 8.9 slice-start.2
  1128.0 7.9 slice-start
  1128.0 8.0 slice-start.1
  1128.0 8.9 slice-start.2
  1157.6 42.0 %copy-start.14 = (bf16[4096,3,64]{0,2,1:T(8,128)(2,1)}, bf16[4096,3,64]{0,2,1:T(8,128)(2,1)S(1)}, u32[]{:S(2)}) copy-start(bf16[4096,3,64]{0,2,1:T(8,128)(2,1)S(1)} %convert.10) | copy-start | bytes 4718596
  1168.4 124.4 %reduce-scatter.25.cloned.1.call-start = ((), (), s32[]{:S(2)}) async-start(), calls=%async_computation.21 | async-start | bytes 884736
  1177.3 188.5 %reduce-scatter.23.cloned.1.call-start = ((), (), s32[]{:S(2)}) async-start(), calls=%async_computation.20 | async-start | bytes 2654208 | tf_op jit(solution)/shard_map/reduce_scatter | solution.py:250
  1188.7 249.9 %reduce-scatter.21.cloned.1.call-start = ((), (), s32[]{:S(2)}) async-start(), calls=%async_computation.19 | async-start | bytes 2654208 | tf_op jit(solution)/shard_map/reduce_scatter | solution.py:249
  1199.4 312.3 %reduce-scatter.19.cloned.1.call-start = ((), (), s32[]{:S(2)}) async-start(), calls=%async_computation.18 | async-start | bytes 2654208 | tf_op jit(solution)/shard_map/reduce_scatter | solution.py:247
  1209.4 17.0 %copy-start.9 = (f32[1024,768]{0,1:T(8,128)S(1)}, f32[1024,768]{0,1:T(8,128)}, u32[]{:S(2)}) copy-start(f32[1024,768]{0,1:T(8,128)} %copy-done.8) | copy-start | bytes 9437188
  1209.4 17.0 %copy-start.25 = (f32[1024]{0:T(1024)S(1)}, f32[1024]{0:T(1024)}, u32[]{:S(2)}) copy-start(f32[1024]{0:T(1024)} %copy-done.24) | copy-start | bytes 12292
  1209.4 302.2 %all-reduce.4.cloned.1.call-start = ((), (), s32[]{:S(2)}) async-start(), calls=%async_computation.22 | async-start | bytes 196608 | tf_op jit(solution)/shard_map/psum | solution.py:261
  1215.0 15.1 copy-start.29
  1215.0 15.1 copy-start.40
  1215.0 17.7 %copy-start.31 = (f32[768]{0:T(1024)S(1)}, f32[768]{0:T(1024)}, u32[]{:S(2)}) copy-start(f32[768]{0:T(1024)} %get-tuple-element.540) | copy-start | bytes 9220
  (68 other events, 284.4 us)
Sparse Core Ops, SparseCore 0:
  15.5 49.0 all-gather.6
  311.7 96.4 reduce-scatter.10
  619.5 46.3 all-gather.14
  804.7 46.3 all-gather.16
  1168.5 57.8 reduce-scatter.16
  1229.6 63.2 reduce-scatter.24
  1296.9 68.8 reduce-scatter.22
  1369.9 68.6 reduce-scatter.20
  1442.7 68.8 reduce-scatter.18
Sparse Core Ops, SparseCore 1:
  314.3 40.7 all-gather.10
  414.3 46.2 all-gather.8
  462.6 41.4 all-gather.12
  514.3 95.4 reduce-scatter.12
  696.4 97.0 reduce-scatter.14
  1232.7 132.7 all-reduce.3
where the time goes:
time: 1530 us
  waiting for transfers between devices  693 us (45%)
  matrix products  468 us (31%)
  other arithmetic  160 us (10%)
  blocking collectives  93.5 us (6%)
  local copies, waits for them, and re-layouts  73 us (5%)
  loops' own time  22.4 us (1%)
  between operations  16.2 us (1%)
    dot_general x16, matrix products, block_inputs(): jnp.einsum('bhe,ghe->hbg', query_rows, key_rows, preferred_element_type=j...  112 us
    reduce_scatter x1, waiting for transfers between devices, shards(): lax.psum_scatter(jnp.einsum('tf,df->td', row_piece, w_up, preferred_eleme...  96.5 us
    reduce_scatter x1, waiting for transfers between devices, shards(): lax.psum_scatter(jnp.einsum('the,dhe->td', row_piece, w_out, preferred_el...  95.4 us
    reduce_scatter x1, waiting for transfers between devices, shards(): lax.psum_scatter(jnp.einsum('tf,df->td', row_piece, w_down, preferred_ele...  92.3 us
    reduce_scatter x1, waiting for transfers between devices, shards(): lax.psum_scatter(grad_qkv, 'dp', scatter_dimension=0, tiled=True)  73 us
    reduce_scatter x1, waiting for transfers between devices, shards(): lax.psum_scatter(grad_up, 'dp', scatter_dimension=0, tiled=True)  72.8 us
    reduce_scatter x1, waiting for transfers between devices, shards(): lax.psum_scatter(grad_down, 'dp', scatter_dimension=0, tiled=True)  67.8 us
    dot_general x8, matrix products, one_block(): jnp.einsum('bhe,ghe->hbg', grad_rows, value_rows, preferred_element_type=...  63.4 us
  transfers between devices with their start and end apart: 15, of which 12 were waited for; matrix products, arithmetic and copies ran while one was open for 7% of the time, Pallas kernels for 0%

commit v1 on v0

v1 whole, which is shorter than its diff:
```python
import jax
import jax.numpy as jnp
from jax import lax
from jax.experimental import pallas as pl
from jax.experimental.pallas import tpu as pltpu
from jax.sharding import PartitionSpec as P

EPSILON = 1e-12
TILE = 256
MASKED = -1e30
VMEM_MAX = 64 * 1024 * 1024 - 128 * 1024
NT = (((1,), (1,)), ((), ()))
NN = (((1,), (0,)), ((), ()))


def mm(a, b, dims=NN):
    return lax.dot_general(a, b, dims, preferred_element_type=jnp.float32)


def fold8(x):
    r = x.shape[0]
    return x.reshape(r // 8, 8, x.shape[1])


def head_masks(block):
    lane = lax.broadcasted_iota(jnp.int32, block.shape, 1)
    zero = jnp.zeros_like(block)
    return jnp.where(lane < 64, block, zero), jnp.where(lane < 64, zero, block)


def tile_visible(first_ref, last_ref, i, t):
    return (first_ref[t] == 0) | ((first_ref[t] <= last_ref[i]) & (last_ref[t] >= first_ref[i]))


def forward_kernel(first_ref, last_ref, q_ref, k_ref, v_ref, kseg_ref, qseg_ref, o_ref, lse_ref,
                   vt_ref, qm_ref, s_ref, m_ref, l_ref, acc_ref):
    i = pl.program_id(0)
    tiles = pl.num_programs(0)
    pairs = q_ref.shape[1] // 128
    heads = 2 * pairs

    @pl.when(i == 0)
    def _():
        def turn(t, c):
            rows = pl.ds(pl.multiple_of(t * TILE, TILE), TILE)
            vt_ref[t] = v_ref[rows, :].T
            return c
        lax.fori_loop(0, tiles, turn, 0)

    for g in range(pairs):
        a, b = head_masks(q_ref[:, 128 * g:128 * g + 128])
        qm_ref[2 * g] = a
        qm_ref[2 * g + 1] = b
    m_ref[...] = jnp.full_like(m_ref, MASKED)
    l_ref[...] = jnp.zeros_like(l_ref)
    acc_ref[...] = jnp.zeros_like(acc_ref)
    qseg = qseg_ref[0:1, :]

    def scores(t, c):
        @pl.when(tile_visible(first_ref, last_ref, i, t))
        def _():
            rows = pl.ds(pl.multiple_of(t * TILE, TILE), TILE)
            kseg = kseg_ref[rows, 0:1]
            seen = (kseg == 0) | (kseg == qseg)
            for h in range(heads):
                kp = k_ref[rows, 128 * (h // 2):128 * (h // 2) + 128]
                s = mm(kp, qm_ref[h], NT)
                s = jnp.where(seen, s, MASKED)
                s_ref[h, t] = s
                m_ref[h] = jnp.maximum(m_ref[h], jnp.max(fold8(s), axis=0))
        return c
    lax.fori_loop(0, tiles, scores, 0)
    for h in range(heads):
        m_ref[h] = jnp.broadcast_to(jnp.max(m_ref[h], axis=0, keepdims=True), (8, TILE))

    def mix(t, c):
        @pl.when(tile_visible(first_ref, last_ref, i, t))
        def _():
            for h in range(heads):
                p = jnp.exp(s_ref[h, t] - m_ref[h, 0:1, :])
                l_ref[h] = l_ref[h] + jnp.sum(fold8(p), axis=0)
                acc_ref[h] = acc_ref[h] + mm(vt_ref[t, 64 * h:64 * h + 64, :], p.astype(jnp.bfloat16))
        return c
    lax.fori_loop(0, tiles, mix, 0)
    for h in range(heads):
        total = jnp.sum(l_ref[h], axis=0, keepdims=True)
        lse_ref[h:h + 1, :] = m_ref[h, 0:1, :] + jnp.log(total)
        acc_ref[h] = acc_ref[h] / total
    for g in range(pairs):
        pair = jnp.concatenate([acc_ref[2 * g], acc_ref[2 * g + 1]], axis=0)
        o_ref[:, 128 * g:128 * g + 128] = pair.T.astype(jnp.bfloat16)


def attend_forward(q, k, v, seg):
    n, width = q.shape
    tiles = n // TILE
    heads = width // 64
    first = seg[::TILE]
    last = seg[TILE - 1::TILE]
    kseg = jnp.broadcast_to(seg[:, None], (n, 128))
    qseg = jnp.broadcast_to(seg[None, :], (8, n))
    whole = lambda shape: pl.BlockSpec(shape, lambda i, *_: (0,) * len(shape))
    return pl.pallas_call(
        forward_kernel,
        out_shape=(jax.ShapeDtypeStruct((n, width), jnp.bfloat16), jax.ShapeDtypeStruct((8, n), jnp.float32)),
        grid_spec=pltpu.PrefetchScalarGridSpec(
            num_scalar_prefetch=2, grid=(tiles,),
            in_specs=[pl.BlockSpec((TILE, width), lambda i, *_: (i, 0)), whole((n, width)), whole((n, width)),
                      whole((n, 128)), pl.BlockSpec((8, TILE), lambda i, *_: (0, i))],
            out_specs=[pl.BlockSpec((TILE, width), lambda i, *_: (i, 0)), pl.BlockSpec((8, TILE), lambda i, *_: (0, i))],
            scratch_shapes=[
                pltpu.VMEM((tiles, width, TILE), jnp.bfloat16),
                pltpu.VMEM((heads, TILE, 128), jnp.bfloat16),
                pltpu.VMEM((heads, tiles, TILE, TILE), jnp.float32),
                pltpu.VMEM((heads, 8, TILE), jnp.float32),
                pltpu.VMEM((heads, 8, TILE), jnp.float32),
                pltpu.VMEM((heads, 64, TILE), jnp.float32),
            ]),
        compiler_params=pltpu.CompilerParams(dimension_semantics=("arbitrary",), vmem_limit_bytes=VMEM_MAX),
        cost_estimate=pl.CostEstimate(flops=4 * n * n * width, bytes_accessed=8 * n * width, transcendentals=n * n * heads),
        name="attend_forward",
    )(first, last, q, k, v, kseg, qseg)


def backward_kernel(first_ref, last_ref, q_ref, do_ref, k_ref, v_ref, kseg_ref, qseg_ref, lse_ref,
                    dq_ref, dk_ref, dv_ref, kt_ref, qm_ref, dom_ref, p_ref, g_ref, delta_ref, dqt_ref, dka_ref, dva_ref):
    i = pl.program_id(0)
    tiles = pl.num_programs(0)
    pairs = q_ref.shape[1] // 128
    heads = 2 * pairs

    @pl.when(i == 0)
    def _():
        def turn(t, c):
            rows = pl.ds(pl.multiple_of(t * TILE, TILE), TILE)
            kt_ref[t] = k_ref[rows, :].T
            dka_ref[rows, :] = jnp.zeros((TILE, 128 * pairs), jnp.float32)
            dva_ref[rows, :] = jnp.zeros((TILE, 128 * pairs), jnp.float32)
            return c
        lax.fori_loop(0, tiles, turn, 0)

    for g in range(pairs):
        a, b = head_masks(q_ref[:, 128 * g:128 * g + 128])
        qm_ref[2 * g] = a
        qm_ref[2 * g + 1] = b
        a, b = head_masks(do_ref[:, 128 * g:128 * g + 128])
        dom_ref[2 * g] = a
        dom_ref[2 * g + 1] = b
    delta_ref[...] = jnp.zeros_like(delta_ref)
    dqt_ref[...] = jnp.zeros_like(dqt_ref)
    qseg = qseg_ref[0:1, :]

    def first_pass(t, c):
        @pl.when(tile_visible(first_ref, last_ref, i, t))
        def _():
            rows = pl.ds(pl.multiple_of(t * TILE, TILE), TILE)
            kseg = kseg_ref[rows, 0:1]
            seen = (kseg == 0) | (kseg == qseg)
            for g in range(pairs):
                cols = slice(128 * g, 128 * g + 128)
                kp = k_ref[rows, cols]
                vp = v_ref[rows, cols]
                part = None
                for h in (2 * g, 2 * g + 1):
                    s = mm(kp, qm_ref[h], NT)
                    p = jnp.where(seen, jnp.exp(s - lse_ref[h:h + 1, :]), 0.0)
                    d = mm(vp, dom_ref[h], NT)
                    p_ref[h, t] = p
                    g_ref[h, t] = d
                    delta_ref[h] = delta_ref[h] + jnp.sum(fold8(p * d), axis=0)
                    one = mm(p.astype(jnp.bfloat16), dom_ref[h])
                    part = one if part is None else part + one
                dva_ref[rows, cols] = dva_ref[rows, cols] + part
        return c
    lax.fori_loop(0, tiles, first_pass, 0)
    for h in range(heads):
        delta_ref[h] = jnp.broadcast_to(jnp.sum(delta_ref[h], axis=0, keepdims=True), (8, TILE))

    def second_pass(t, c):
        @pl.when(tile_visible(first_ref, last_ref, i, t))
        def _():
            rows = pl.ds(pl.multiple_of(t * TILE, TILE), TILE)
            for g in range(pairs):
                cols = slice(128 * g, 128 * g + 128)
                part = None
                for h in (2 * g, 2 * g + 1):
                    ds = (p_ref[h, t] * (g_ref[h, t] - delta_ref[h, 0:1, :])).astype(jnp.bfloat16)
                    one = mm(ds, qm_ref[h])
                    part = one if part is None else part + one
                    dqt_ref[h] = dqt_ref[h] + mm(kt_ref[t, 64 * h:64 * h + 64, :], ds)
                dka_ref[rows, cols] = dka_ref[rows, cols] + part
        return c
    lax.fori_loop(0, tiles, second_pass, 0)
    for g in range(pairs):
        pair = jnp.concatenate([dqt_ref[2 * g], dqt_ref[2 * g + 1]], axis=0)
        dq_ref[:, 128 * g:128 * g + 128] = (pair.T * 0.125).astype(jnp.bfloat16)

    @pl.when(i == tiles - 1)
    def _():
        dk_ref[...] = dka_ref[...].astype(jnp.bfloat16)
        dv_ref[...] = dva_ref[...].astype(jnp.bfloat16)


def attend_backward(q, k, v, do, lse, seg):
    n, width = q.shape
    tiles = n // TILE
    heads = width // 64
    first = seg[::TILE]
    last = seg[TILE - 1::TILE]
    kseg = jnp.broadcast_to(seg[:, None], (n, 128))
    qseg = jnp.broadcast_to(seg[None, :], (8, n))
    whole = lambda shape: pl.BlockSpec(shape, lambda i, *_: (0,) * len(shape))
    rows = pl.BlockSpec((TILE, width), lambda i, *_: (i, 0))
    stat = pl.BlockSpec((8, TILE), lambda i, *_: (0, i))
    out = jax.ShapeDtypeStruct((n, width), jnp.bfloat16)
    return pl.pallas_call(
        backward_kernel,
        out_shape=(out, out, out),
        grid_spec=pltpu.PrefetchScalarGridSpec(
            num_scalar_prefetch=2, grid=(tiles,),
            in_specs=[rows, rows, whole((n, width)), whole((n, width)), whole((n, 128)), stat, stat],
            out_specs=[rows, whole((n, width)), whole((n, width))],
            scratch_shapes=[
                pltpu.VMEM((tiles, width, TILE), jnp.bfloat16),
                pltpu.VMEM((heads, TILE, 128), jnp.bfloat16),
                pltpu.VMEM((heads, TILE, 128), jnp.bfloat16),
                pltpu.VMEM((heads, tiles, TILE, TILE), jnp.float32),
                pltpu.VMEM((heads, tiles, TILE, TILE), jnp.float32),
                pltpu.VMEM((heads, 8, TILE), jnp.float32),
                pltpu.VMEM((heads, 64, TILE), jnp.float32),
                pltpu.VMEM((n, width), jnp.float32),
                pltpu.VMEM((n, width), jnp.float32),
            ]),
        compiler_params=pltpu.CompilerParams(dimension_semantics=("arbitrary",), vmem_limit_bytes=VMEM_MAX),
        cost_estimate=pl.CostEstimate(flops=10 * n * n * width, bytes_accessed=14 * n * width, transcendentals=n * n * heads),
        name="attend_backward",
    )(first, last, q, do, k, v, kseg, qseg, lse)


def layer_norm(values, norm_gain, norm_shift):
    centre = values - jnp.mean(values, axis=-1, keepdims=True)
    spread = jnp.mean(centre * centre, axis=-1, keepdims=True)
    return centre * lax.rsqrt(spread + EPSILON) * norm_gain + norm_shift


def gelu_exact(values):
    return jax.nn.gelu(values, approximate=False)


AXES = ("dp", "tensor")


class Grid:
    def __init__(self, dp, tensor):
        self.dp, self.tensor = dp, tensor
        factors, rest = [2], dp // 2
        while rest > 8:
            factors.insert(0, 4)
            rest //= 4
        if rest > 1:
            factors.insert(0, rest)
        self.factors = factors

    def digit(self, j):
        stride = 1
        for f in self.factors[j + 1:]:
            stride *= f
        return stride, self.factors[j]

    def my_digit(self, j):
        stride, f = self.digit(j)
        return lax.axis_index("dp") // stride % f

    def turn(self, value, j, k):
        stride, f = self.digit(j)
        pairs = []
        for d in range(self.dp):
            g = d // stride % f
            to = d + ((g + k) % f - g) * stride
            for t in range(self.tensor):
                pairs.append((d * self.tensor + t, to * self.tensor + t))
        return lax.ppermute(value, AXES, pairs)

    def swap_dp(self, value, bit):
        pairs = [(d * self.tensor + t, (d ^ bit) * self.tensor + t) for d in range(self.dp) for t in range(self.tensor)]
        return lax.ppermute(value, AXES, pairs)

    def swap(self, value, bit):
        pairs = [(d * self.tensor + t, d * self.tensor + (t ^ bit)) for d in range(self.dp) for t in range(self.tensor)]
        return lax.ppermute(value, AXES, pairs)

    def gather_stage(self, value, j, axis):
        _, f = self.digit(j)
        g = self.my_digit(j)
        got = [value] + [self.turn(value, j, k) for k in range(1, f)]
        if f == 2:
            lower = jnp.where(g == 0, got[0], got[1])
            upper = jnp.where(g == 0, got[1], got[0])
            return jnp.stack([lower, upper], axis=axis)
        ring = got[::-1]
        return lax.dynamic_slice_in_dim(jnp.stack(ring + ring[:-1], axis=axis), f - 1 - g, f, axis)

    def gather(self, shard, outer_first=False):
        count = len(self.factors)
        value = shard
        for j in range(count - 1):
            value = self.gather_stage(value, j, j)
        if outer_first:
            value = jnp.stack([value, self.swap(value, 2)])
            value = self.gather_stage(value, count - 1, count)
            return value.reshape(2, -1, shard.shape[-1])
        value = self.gather_stage(value, count - 1, count - 1)
        value = value.reshape(-1, shard.shape[-1])
        return jnp.stack([value, self.swap(value, 2)])

    def reduce_stage(self, value, j, axis):
        _, f = self.digit(j)
        g = self.my_digit(j)
        total = lax.dynamic_index_in_dim(value, g, axis, keepdims=False).astype(jnp.float32)
        for k in range(1, f):
            part = lax.dynamic_index_in_dim(value, (g + k) % f, axis, keepdims=False)
            total = total + self.turn(part.astype(jnp.bfloat16), j, k).astype(jnp.float32)
        return total

    def reduce(self, parts, outer_first=True):
        count = len(self.factors)
        columns = parts.shape[-1]
        value = parts
        if outer_first:
            value = value[0].astype(jnp.float32) + self.swap(value[1].astype(jnp.bfloat16), 2).astype(jnp.float32)
            value = value.reshape(*self.factors, -1, columns)
            value = self.reduce_stage(value, count - 1, count - 1)
        else:
            value = value.reshape(2, *self.factors, -1, columns)
            value = self.reduce_stage(value, count - 1, count)
            value = value[0] + self.swap(value[1].astype(jnp.bfloat16), 2).astype(jnp.float32)
        for j in reversed(range(count - 1)):
            value = self.reduce_stage(value, j, j)
        return value

    def total(self, vector):
        for bit in (1, 2):
            vector = vector + self.swap(vector, bit)
        bit = 1
        while bit < self.dp:
            vector = vector + self.swap_dp(vector, bit)
            bit *= 2
        return vector


def shards(grid, tokens, segment_ids, memory_positions, memory_rows, qkv_weight, qv_bias, out_weight, out_bias,
           norm1_gain, norm1_bias, up_weight, up_bias, down_weight, down_bias, norm2_gain, norm2_bias, out_cotangent):
    f32, bf16 = jnp.float32, jnp.bfloat16
    rows, width = tokens.shape
    group_len = segment_ids.shape[1]
    tensor = lax.axis_index("tensor")
    inner, outer = tensor % 2, tensor // 2
    slice_rows = qkv_weight.shape[0]
    heads = qkv_weight.shape[1]
    hd = 64
    hw = heads * hd
    units = up_weight.shape[1]

    segments = lax.dynamic_index_in_dim(segment_ids, outer, 0, keepdims=False)
    positions = lax.dynamic_index_in_dim(memory_positions, outer, 0, keepdims=False)
    row_place = inner * rows + jnp.arange(rows, dtype=jnp.int32)
    picks = (row_place[:, None] == positions[None, :])
    x0 = tokens.astype(f32) + jnp.dot(picks.astype(bf16), memory_rows, preferred_element_type=f32)
    xl = x0.astype(bf16)

    shard_qkv = qkv_weight.reshape(slice_rows, heads, 3, hd).transpose(0, 2, 1, 3).reshape(slice_rows, 3 * hw)
    w_qkv = grid.gather(shard_qkv)
    w_qkv = w_qkv.reshape(2, width, 3, hw).transpose(1, 2, 0, 3).reshape(width, 6 * hw)
    other = grid.swap(xl, 1)
    x_all = jnp.concatenate([jnp.where(inner == 0, xl, other), jnp.where(inner == 0, other, xl)])
    w_out = grid.gather(out_weight.reshape(slice_rows, hw), True)
    w_up = grid.gather(up_weight)
    w_down = grid.gather(down_weight, True)

    small = jnp.concatenate([qv_bias.reshape(-1), up_bias])
    small_other = grid.swap(small, 2)
    qv = jnp.stack([small[:2 * hw], small_other[:2 * hw]]).reshape(2, heads, 2, hd).astype(f32)
    b_up = jnp.concatenate([small[2 * hw:], small_other[2 * hw:]])
    b_up = jnp.stack([b_up, grid.swap(b_up, 1)]).astype(f32)
    b_qkv = jnp.stack([qv[:, :, 0], jnp.zeros_like(qv[:, :, 0]), qv[:, :, 1]], 0).reshape(6 * hw)

    joined = lambda w: w.transpose(1, 0, 2).reshape(width, -1)
    w_out, w_up, w_down = joined(w_out), joined(w_up), joined(w_down)
    w_out = (w_out, grid.swap(w_out, 1))
    w_up = (w_up, grid.swap(w_up, 1))
    w_down = (w_down, grid.swap(w_down, 1))

    qkv = (jnp.dot(x_all, w_qkv, preferred_element_type=f32) + b_qkv).astype(bf16)
    q = qkv[:, :2 * hw] * jnp.asarray(0.125, bf16)
    k = qkv[:, 2 * hw:4 * hw]
    v = qkv[:, 4 * hw:]
    mixed, lse = attend_forward(q, k, v, segments)
    halves = mixed.reshape(2, rows, 2 * hw)
    o_own = lax.dynamic_index_in_dim(halves, inner, 0, keepdims=False)
    o_got = grid.swap(lax.dynamic_index_in_dim(halves, 1 - inner, 0, keepdims=False), 1)
    o = (o_own, o_got)

    attended = out_bias.astype(f32)
    for side in range(2):
        attended = attended + mm(o[side], w_out[side], NT)
    r1 = x0 + attended
    g1, s1 = norm1_gain.astype(f32), norm1_bias.astype(f32)
    g2, s2 = norm2_gain.astype(f32), norm2_bias.astype(f32)
    h1 = layer_norm(r1, g1, s1)
    hl = h1.astype(bf16)
    u = [mm(hl, w_up[side]) + b_up[side] for side in range(2)]
    z = [gelu_exact(one).astype(bf16) for one in u]
    r2 = h1 + down_bias.astype(f32)
    for side in range(2):
        r2 = r2 + mm(z[side], w_down[side], NT)
    block_out = layer_norm(r2, g2, s2).astype(bf16)
    cot = out_cotangent.astype(f32)
    dr2, dg2, ds2 = jax.vjp(layer_norm, r2, g2, s2)[1](cot)
    dfl = dr2.astype(bf16)
    d_down_bias = jnp.sum(dfl.astype(f32), axis=0)
    TN = (((0,), (0,)), ((), ()))
    g_down = [mm(dfl, z[side], TN) for side in range(2)]
    dul = [jax.vjp(gelu_exact, u[side])[1](mm(dfl, w_down[side]))[0].astype(bf16) for side in range(2)]
    g_up = [mm(hl, dul[side], TN) for side in range(2)]
    d_up_bias = [jnp.sum(dul[side].astype(f32), axis=0) for side in range(2)]
    dh1 = dr2
    for side in range(2):
        dh1 = dh1 + mm(dul[side], w_up[side], NT)
    dr1, dg1, ds1 = jax.vjp(layer_norm, r1, g1, s1)[1](dh1)
    dal = dr1.astype(bf16)
    d_out_bias = jnp.sum(dal.astype(f32), axis=0)
    g_out = [mm(dal, o[side], TN) for side in range(2)]
    dol = [mm(dal, w_out[side]).astype(bf16) for side in range(2)]
    got = grid.swap(dol[1], 1)
    do_all = jnp.concatenate([jnp.where(inner == 0, dol[0], got), jnp.where(inner == 0, got, dol[0])])

    def spread(pair, outer_first):
        own = pair[0] + grid.swap(pair[1].astype(bf16), 1).astype(f32)
        own = own.reshape(width, 2, -1).transpose(1, 0, 2)
        return grid.reduce(own, outer_first)

    grad_down = spread(g_down, True)
    grad_up = spread(g_up, False)
    grad_out = spread(g_out, True)

    dq, dk, dv = attend_backward(q, k, v, do_all, lse, segments)
    d_qkv = jnp.concatenate([dq, dk, dv], axis=-1)
    g_qkv = mm(x_all, d_qkv, TN)
    d_bias = jnp.sum(d_qkv.astype(f32), axis=0).reshape(3, 2, hw)
    part = mm(d_qkv, w_qkv, NT).reshape(2, rows, width)
    mine = lax.dynamic_index_in_dim(part, inner, 0, keepdims=False)
    theirs = lax.dynamic_index_in_dim(part, 1 - inner, 0, keepdims=False).astype(bf16)
    grad_tokens = mine + grid.swap(theirs, 1).astype(f32) + dr1
    grad_qkv = grid.reduce(g_qkv.reshape(width, 3, 2, hw).transpose(2, 0, 1, 3).reshape(2, width, 3 * hw), True)
    grad_qkv = grad_qkv.reshape(slice_rows, 3, heads, hd).transpose(0, 2, 1, 3).reshape(slice_rows, heads, 3 * hd)
    grad_memory = jnp.dot(picks.astype(f32).T, grad_tokens, precision=lax.Precision.HIGHEST)

    order = jnp.arange(4, dtype=jnp.int32) ^ tensor
    up_parts = jnp.concatenate(d_up_bias).reshape(2, 2, units).transpose(0, 1, 2)
    up_parts = jnp.stack([up_parts[0, 0], up_parts[1, 0], up_parts[0, 1], up_parts[1, 1]])[order]
    nothing = jnp.zeros_like(d_bias[0, 0])
    take = lambda o_: jnp.stack([d_bias[0, o_].reshape(heads, hd), d_bias[2, o_].reshape(heads, hd)], 1).reshape(-1)
    blank = jnp.zeros((2 * hw,), f32)
    qv_parts = jnp.stack([take(0), blank, take(1), blank])[order]
    pieces = [grad_memory.reshape(-1), d_out_bias, dg1, ds1, d_down_bias, dg2, ds2, up_parts.reshape(-1), qv_parts.reshape(-1)]
    summed = grid.total(jnp.concatenate(pieces))
    outs, at = [], 0
    for piece in pieces:
        outs.append(lax.slice_in_dim(summed, at, at + piece.size))
        at += piece.size
    t_memory, t_out_bias, t_g1, t_s1, t_down_bias, t_g2, t_s2, t_up, t_qv = outs
    grad_up_bias = lax.dynamic_index_in_dim(t_up.reshape(4, units), tensor, 0, keepdims=False)
    grad_qv = lax.dynamic_index_in_dim(t_qv.reshape(4, heads, 2 * hd), tensor, 0, keepdims=False)
    return (block_out, grad_tokens, t_memory.reshape(-1, width), grad_qkv, grad_qv,
            grad_out.reshape(slice_rows, heads, hd), t_out_bias, t_g1, t_s1, grad_up, grad_up_bias, grad_down,
            t_down_bias, t_g2, t_s2)


def solution(mesh):
    grid = Grid(mesh.shape["dp"], mesh.shape["tensor"])
    tokens, dp, none = P(AXES, None), P("dp", None), P()
    heads, matrix = P("dp", "tensor", None), P("dp", "tensor")
    in_specs = (tokens, dp, dp, none, heads, P("tensor", None), heads, none, none, none, matrix, P("tensor"), matrix,
                none, none, none, tokens)
    out_specs = (tokens, tokens, none, heads, P("tensor", None), heads, none, none, none, matrix, P("tensor"), matrix,
                 none, none, none)

    def run(*args):
        return shards(grid, *args)

    return jax.shard_map(run, mesh=mesh, in_specs=in_specs, out_specs=out_specs, check_vma=False)
```

time: 1530 us -> 548 us (0.36)
  waiting for transfers between devices: 693 us -> 70.6 us
  matrix products: 468 us -> 124 us
  Pallas kernels: 0 us -> 118 us
  other arithmetic: 160 us -> 53.9 us
  blocking collectives: 93.5 us -> 0 us
  starting transfers between devices: 1.5 us -> 67.5 us
  local copies, waits for them, and re-layouts: 73 us -> 105 us
  loops' own time: 22.4 us -> 0 us
    reduce_scatter x7 -> x0, waiting for transfers between devices: 509 us -> none  [the longest x1 96.5 us: shards(): lax.psum_scatter(jnp.einsum('tf,df->td', row_piece, w_up, preferred_eleme...]
    dot_general x67 -> x23, matrix products: 452 us -> 124 us  [the longest x20 115 us: mm(): return lax.dot_general(a, b, dims, preferred_element_type=jnp.float32)]
    all_gather x6 -> x0, waiting for transfers between devices: 145 us -> none  [the longest x1 46.3 us: shards(): lax.all_gather(grad_branch_low, 'tensor', axis=0, tiled=True)]
    pallas_call x0 -> x2, Pallas kernels: none -> 118 us  [the longest x1 76.4 us: attend_backward(): pl.pallas_call(backward_kernel, out_shape=(out, out, out), grid_spec=pltp...]
    all_gather x2 -> x0, blocking collectives: 71.3 us -> none  [the longest x1 39 us: shards(): lax.all_gather(qkv_weight, 'dp', axis=0, tiled=True)]
    ppermute x0 -> x57, waiting for transfers between devices: none -> 70.6 us  [the longest x32 47.5 us: turn(): return lax.ppermute(value, AXES, pairs)]
    ppermute x0 -> x57, starting transfers between devices: none -> 67.5 us  [the longest x32 49.8 us: turn(): return lax.ppermute(value, AXES, pairs)]
    reduce_sum x12 -> x3, other arithmetic: 63 us -> 4.09 us  [the longest x1 3.04 us: shards(): d_down_bias = jnp.sum(dfl.astype(f32), axis=0)]
  transfers between devices with their start and end apart: 15 -> 57, of which waited for: 12 -> 15; matrix products, arithmetic and copies ran while one was open for 7% -> 40% of each run, Pallas kernels for 0% -> 22%
where the time goes in v1:
time: 548 us; the launch traced here: 542 us
  matrix products  124 us (23%)
  Pallas kernels  118 us (22%)
  local copies, waits for them, and re-layouts  105 us (19%)
  waiting for transfers between devices  70.6 us (13%)
  starting transfers between devices  67.5 us (12%)
  other arithmetic  53.9 us (10%)
    dot_general x20, matrix products, mm(): return lax.dot_general(a, b, dims, preferred_element_type=jnp.float32)  115 us
    pallas_call x1, Pallas kernels, attend_backward(): pl.pallas_call(backward_kernel, out_shape=(out, out, out), grid_spec=pltp...  76.4 us
    ppermute x32, starting transfers between devices, turn(): return lax.ppermute(value, AXES, pairs)  49.8 us
    ppermute x32, waiting for transfers between devices, turn(): return lax.ppermute(value, AXES, pairs)  47.5 us
    pallas_call x1, Pallas kernels, attend_forward(): pl.pallas_call(forward_kernel, out_shape=(jax.ShapeDtypeStruct((n, width)...  41.8 us
    unnamed x192, local copies, waits for them, and re-layouts  36 us
    ppermute x3, waiting for transfers between devices, swap_dp(): return lax.ppermute(value, AXES, pairs)  15.4 us
    ppermute x22, starting transfers between devices, swap(): return lax.ppermute(value, AXES, pairs)  12.6 us
  transfers between devices with their start and end apart: 57, of which 15 were waited for; matrix products, arithmetic and copies ran while one was open for 40% of the time, Pallas kernels for 22%

profile of v1, /device:TPU:0, one launch (start us, length us, event | category | flops | bytes accessed | tf_op | source)
XLA Modules:
  0.0 542.4 jit_solution(16221819335674539615)
XLA Ops:
  1.8 5.1 collective-permute-start.1
  10.2 2.8 collective-permute-start.7
  20.6 2.7 copy.173
  27.8 5.9 %collective-permute-done.9 = bf16[96,192]{0,1:T(8,128)(2,1)S(1)} collective-permute-done((bf16[96,192]{0,1:T(8,128)(2,1)S(1)}, bf16[96,192]{0,1:T(8,128)(2,1)S(1)}, u32[]{:S(2)}, u32[]{:S(2)}) %collective-permute-start.9) | collective-permute-done | bytes 36896 | tf_op jit(solution)/shard_map/ppermute | solution.py:282
  55.1 4.5 collective-permute-done.21
  75.5 11.9 %collective-permute-done.11 = bf16[2,4,96,192]{2,3,1,0:T(8,128)(2,1)} collective-permute-done((bf16[2,4,96,192]{2,3,1,0:T(8,128)(2,1)}, bf16[2,4,96,192]{2,3,1,0:T(8,128)(2,1)}, u32[]{:S(2)}, u32[]{:S(2)}) %collective-permute-start.11) | collective-permute-done | bytes 294944 | tf_op jit(solution)/shard_map/ppermute | solution.py:282
  90.4 3.6 reshape.284
  96.3 4.1 stack.173
  111.9 5.1 add_convert_fusion
  121.3 41.8 %attend_forward.1 = (bf16[2048,384]{1,0:T(8,128)(2,1)}, f32[8,2048]{1,0:T(8,128)}) custom-call(s32[8]{0:T(128)} %slice.156.first_ref, s32[8]{0:T(128)} %slice.157.last_ref, bf16[2048,384]{1,0:T(8,128)(2,1)} %get-tuple-element.130.q_ref, bf16[2048,384]{1,0:T(8,128)(2,1)} %get-tuple-element.129.k_ref, bf16[2048,384]{1,0:T(8,128)(2,1)} %get-tuple-element.128.v_ref, ...), custom_call_target="tpu_custom_call" | custom-call | flops 6442450944 | bytes 6291456 | tf_op jit(solution)/shard_map/attend_forward/pallas_call | solution.py:103
  165.1 4.0 fusion.26
  178.3 5.1 fusion.79
  185.9 18.8 %multiply_convert_fusion.1 = (bf16[1024,1536]{1,0:T(8,128)(2,1)S(1)}, f32[1024,1536]{1,0:T(8,128)}, f32[1024,1536]{1,0:T(8,128)}) fusion(f32[1536]{0:T(1024)S(1)} %get-tuple-element.109, bf16[1024,768]{0,1:T(8,128)(2,1)S(1)} %fusion.17, bf16[768,1536]{0,1:T(8,128)(2,1)S(1)} %bitcast.306), kind=kOutput, calls=%fused_computation.25 | convolution fusion | flops 2519728128 | bytes 19666944 | tf_op jit(solution)/shard_map/dot_general | solution.py:17
  204.7 2.7 fusion.81
  207.4 19.8 %multiply_convert_fusion = (bf16[1024,1536]{1,0:T(8,128)(2,1)S(1)}, f32[1024,1536]{1,0:T(8,128)}, f32[1024,1536]{1,0:T(8,128)}) fusion(f32[1536]{0:T(1024)S(1)} %get-tuple-element.108, bf16[1024,768]{0,1:T(8,128)(2,1)S(1)} %fusion.17, bf16[768,1536]{0,1:T(8,128)(2,1)} %collective-permute-done.25), kind=kOutput, calls=%fused_computation.12 | convolution fusion | flops 2519728128 | bytes 19666944 | tf_op jit(solution)/shard_map/dot_general | solution.py:17
  227.3 3.5 fusion.80
  233.6 3.0 convert_reduce_fusion.4
  236.6 3.0 copy.188
  239.6 6.5 %convolution_convert_fusion = bf16[768,1536]{1,0:T(8,128)(2,1)} fusion(bf16[1024,768]{0,1:T(8,128)(2,1)} %get-tuple-element.119, bf16[1024,1536]{1,0:T(8,128)(2,1)} %copy-done.72), kind=kOutput, calls=%fused_computation.51 | convolution fusion | flops 2417098752 | bytes 7077888 | tf_op jit(solution)/shard_map/dot_general | solution.py:17
  246.1 7.7 %convert_reduce_fusion.2 = (f32[1536]{0:T(1024)S(1)}, bf16[1024,1536]{1,0:T(8,128)(2,1)S(1)}) fusion(f32[1024,1536]{1,0:T(8,128)} %get-tuple-element.127, f32[1024,1536]{1,0:T(8,128)} %get-tuple-element.174, f32[1536]{0:T(1024)S(1)} %copy-done.54, bf16[1024,768]{0,1:T(8,128)(2,1)S(1)} %copy-done.37, bf16[768,1536]{0,1:T(8,128)(2,1)S(1)} %bitcast.310), kind=kOutput, calls=%fused_computation.9 | convolution fusion | flops 2442656256 | bytes 19673088 | tf_op jit(solution)/shard_map/dot_general | solution.py:17
  253.9 2.7 fusion.82
  256.7 6.8 %convert_reduce_fusion.1 = (f32[1536]{0:T(1024)S(1)}, bf16[1024,1536]{1,0:T(8,128)(2,1)S(1)}) fusion(f32[1024,1536]{1,0:T(8,128)S(1)} %bitcast.340, f32[1024,1536]{1,0:T(8,128)} %get-tuple-element.175, f32[1536]{0:T(1024)S(1)} %get-tuple-element.108, bf16[1024,768]{0,1:T(8,128)(2,1)S(1)} %copy-done.37, bf16[768,1536]{0,1:T(8,128)(2,1)S(1)} %copy-done.67), kind=kOutput, calls=%fused_computation.8 | convolution fusion | flops 2442656256 | bytes 19673088 | tf_op jit(solution)/shard_map/dot_general | solution.py:17
  263.6 3.9 convolution_convert_fusion.1
  267.5 6.3 %multiply_reduce_fusion = (f32[768]{0:T(1024)S(1)}, f32[1024]{0:T(1024)S(1)}, f32[768]{0:T(1024)S(1)}, f32[1024,768]{0,1:T(8,128)S(1)}) fusion(f32[1024,768]{0,1:T(8,128)S(1)} %get-tuple-element.173, f32[1024]{0:T(1024)S(1)} %fusion.65, f32[1024]{0:T(1024)S(1)} %broadcast_multiply_fusion.1, f32[768]{0:T(1024)S(1)} %convert_element_type.287, ...), kind=kOutput, calls=%fused_computation.59 | convolution fusion | flops 2430072320 | bytes 19701760 | tf_op jit(solution)/shard_map/dot_general | solution.py:17
  275.0 3.4 convolution_convert_fusion.2
  287.8 76.4 %attend_backward.1 = (bf16[2048,384]{1,0:T(8,128)(2,1)}, bf16[2048,384]{1,0:T(8,128)(2,1)}, bf16[2048,384]{1,0:T(8,128)(2,1)}) custom-call(s32[8]{0:T(128)} %slice.156.first_ref, s32[8]{0:T(128)} %slice.157.last_ref, bf16[2048,384]{1,0:T(8,128)(2,1)} %get-tuple-element.130.q_ref, bf16[2048,384]{1,0:T(8,128)(2,1)} %pad_maximum_fusion.4.do_ref, ...), custom_call_target="tpu_custom_call" | custom-call | flops 16106127360 | bytes 11010048 | tf_op jit(solution)/shard_map/attend_backward/pallas_call | solution.py:216
  368.7 6.0 %fusion.20 = f32[768,1152]{0,1:T(8,128)} fusion(bf16[2048,1152]{1,0:T(8,128)(2,1)S(1)} %constant_dynamic-update-slice_fusion.8, bf16[1024,768]{0,1:T(8,128)(2,1)S(1)} %copy-done.42, bf16[1024,768]{0,1:T(8,128)(2,1)S(1)} %copy-done.40), kind=kOutput, calls=%fused_computation.81 | convolution fusion | flops 3630170112 | bytes 11403264 | tf_op jit(solution)/shard_map/dot_general | solution.py:17
  374.7 4.4 fusion.83
  379.1 2.6 copy-done.21
  384.8 2.6 slice.265
  391.4 3.0 reshape.299
  397.0 2.8 slice.217
  406.3 3.0 collective-permute-done.34
  409.4 5.6 %collective-permute-start.43 = (bf16[96,192]{0,1:T(8,128)(2,1)S(1)}, bf16[96,192]{0,1:T(8,128)(2,1)S(1)}, u32[]{:S(2)}, u32[]{:S(2)}) collective-permute-start(bf16[96,192]{0,1:T(8,128)(2,1)S(1)} %get-tuple-element.155), channel_id=1, source_target_pairs={{0,16},{1,17},{2,18},{3,19},{4,20},{5,21},{6,22},{7,23},{8,24},{9,... | collective-permute-start | bytes 110600 | tf_op jit(solution)/shard_map/ppermute | solution.py:282
  414.9 2.7 bitcast_add_fusion.2
  417.7 2.9 copy.180
  423.8 3.3 fusion.16
  430.8 5.2 convert_add_fusion.1
  440.5 4.3 convert_add_fusion
  453.4 15.0 %collective-permute-done.31 = f32[24576]{0:T(1024)S(1)} collective-permute-done((f32[24576]{0:T(1024)S(1)}, f32[24576]{0:T(1024)S(1)}, u32[]{:S(2)}, u32[]{:S(2)}) %collective-permute-start.31) | collective-permute-done | bytes 98336 | tf_op jit(solution)/shard_map/ppermute | solution.py:286
  469.1 3.3 collective-permute-start.38
  477.7 4.3 collective-permute-start.33
  482.0 5.9 %collective-permute-done.37 = bf16[96,576]{1,0:T(8,128)(2,1)S(1)} collective-permute-done((bf16[96,576]{1,0:T(8,128)(2,1)S(1)}, bf16[96,576]{1,0:T(8,128)(2,1)S(1)}, u32[]{:S(2)}, u32[]{:S(2)}) %collective-permute-start.37) | collective-permute-done | bytes 110624 | tf_op jit(solution)/shard_map/ppermute | solution.py:282
  510.3 2.8 collective-permute-start.50
  513.1 2.9 collective-permute-start.49
  521.1 4.9 collective-permute-start.54
  526.0 10.4 %collective-permute-done.49 = bf16[96,768]{1,0:T(8,128)(2,1)S(1)} collective-permute-done((bf16[96,768]{1,0:T(8,128)(2,1)S(1)}, bf16[96,768]{1,0:T(8,128)(2,1)S(1)}, u32[]{:S(2)}, u32[]{:S(2)}) %collective-permute-start.49) | collective-permute-done | bytes 147488 | tf_op jit(solution)/shard_map/ppermute | solution.py:282
  537.2 3.9 collective-permute-done.55
  (445 shorter events, 176.5 us)
Async XLA Ops:
  1.8 33.4 %collective-permute-start.1 = (bf16[96,576]{0,1:T(8,128)(2,1)S(1)}, bf16[96,576]{0,1:T(8,128)(2,1)S(1)}, u32[]{:S(2)}, u32[]{:S(2)}) collective-permute-start(bf16[96,576]{0,1:T(8,128)(2,1)S(1)} %bitcast.322), channel_id=1, source_target_pairs={{0,24},{1,25},{2,26},{3,27},{4,28},{5,29},{6,30},{7,31},{8,0},{9,1... | collective-permute-start | bytes 331784 | tf_op jit(solution)/shard_map/ppermute | solution.py:282
  6.9 30.0 %collective-permute-start.2 = (bf16[96,576]{0,1:T(8,128)(2,1)S(1)}, bf16[96,576]{0,1:T(8,128)(2,1)}, u32[]{:S(2)}, u32[]{:S(2)}) collective-permute-start(bf16[96,576]{0,1:T(8,128)(2,1)S(1)} %bitcast.323), channel_id=1, source_target_pairs={{0,16},{1,17},{2,18},{3,19},{4,20},{5,21},{6,22},{7,23},{8,24},{9,... | collective-permute-start | bytes 331784 | tf_op jit(solution)/shard_map/ppermute | solution.py:282
  6.9 33.4 %collective-permute-start.3 = (bf16[96,576]{0,1:T(8,128)(2,1)S(1)}, bf16[96,576]{0,1:T(8,128)(2,1)}, u32[]{:S(2)}, u32[]{:S(2)}) collective-permute-start(bf16[96,576]{0,1:T(8,128)(2,1)S(1)} %bitcast.324), channel_id=1, source_target_pairs={{0,8},{1,9},{2,10},{3,11},{4,12},{5,13},{6,14},{7,15},{8,16},{9,17... | collective-permute-start | bytes 331784 | tf_op jit(solution)/shard_map/ppermute | solution.py:282
  8.6 16.6 %collective-permute-start.6 = (bf16[1152]{0:T(1024)(128)(2,1)S(1)}, bf16[1152]{0:T(1024)(128)(2,1)S(1)}, u32[]{:S(2)}, u32[]{:S(2)}) collective-permute-start(bf16[1152]{0:T(1024)(128)(2,1)S(1)} %pad_maximum_fusion.13), channel_id=1, source_target_pairs={{0,2},{1,3},{2,0},{3,1},{4,6},{5,7},{6,4},{7,5},{8,10},{9,11},{10,... | collective-permute-start | bytes 6920 | tf_op jit(solution)/shard_map/ppermute | solution.py:290
  10.2 17.6 %collective-permute-start.7 = (bf16[96,192]{0,1:T(8,128)(2,1)}, bf16[96,192]{0,1:T(8,128)(2,1)S(1)}, u32[]{:S(2)}, u32[]{:S(2)}) collective-permute-start(bf16[96,192]{0,1:T(8,128)(2,1)} %bitcast.334), channel_id=1, source_target_pairs={{0,24},{1,25},{2,26},{3,27},{4,28},{5,29},{6,30},{7,31},{8,0},{9,1... | collective-permute-start | bytes 110600 | tf_op jit(solution)/shard_map/ppermute | solution.py:282
  33.7 12.2 %collective-permute-start.14 = (bf16[96,768]{1,0:T(8,128)(2,1)S(1)}, bf16[96,768]{1,0:T(8,128)(2,1)S(1)}, u32[]{:S(2)}, u32[]{:S(2)}) collective-permute-start(bf16[96,768]{1,0:T(8,128)(2,1)S(1)} %copy-done.45), channel_id=1, source_target_pairs={{0,24},{1,25},{2,26},{3,27},{4,28},{5,29},{6,30},{7,31},{8,0},{9,1... | collective-permute-start | bytes 442376 | tf_op jit(solution)/shard_map/ppermute | solution.py:282
  33.9 15.3 %collective-permute-start.15 = (bf16[96,768]{1,0:T(8,128)(2,1)S(1)}, bf16[96,768]{1,0:T(8,128)(2,1)S(1)}, u32[]{:S(2)}, u32[]{:S(2)}) collective-permute-start(bf16[96,768]{1,0:T(8,128)(2,1)S(1)} %copy-done.45), channel_id=1, source_target_pairs={{0,16},{1,17},{2,18},{3,19},{4,20},{5,21},{6,22},{7,23},{8,24},{9,... | collective-permute-start | bytes 442376 | tf_op jit(solution)/shard_map/ppermute | solution.py:282
  35.2 14.0 %collective-permute-start.16 = (bf16[96,768]{1,0:T(8,128)(2,1)S(1)}, bf16[96,768]{1,0:T(8,128)(2,1)}, u32[]{:S(2)}, u32[]{:S(2)}) collective-permute-start(bf16[96,768]{1,0:T(8,128)(2,1)S(1)} %copy-done.45), channel_id=1, source_target_pairs={{0,8},{1,9},{2,10},{3,11},{4,12},{5,13},{6,14},{7,15},{8,16},{9,17... | collective-permute-start | bytes 442376 | tf_op jit(solution)/shard_map/ppermute | solution.py:282
  36.9 15.7 %collective-permute-start.20 = (bf16[96,768]{1,0:T(8,128)(2,1)}, bf16[96,768]{1,0:T(8,128)(2,1)S(1)}, u32[]{:S(2)}, u32[]{:S(2)}) collective-permute-start(bf16[96,768]{1,0:T(8,128)(2,1)} %param.29), channel_id=1, source_target_pairs={{0,24},{1,25},{2,26},{3,27},{4,28},{5,29},{6,30},{7,31},{8,0},{9,1... | collective-permute-start | bytes 442376 | tf_op jit(solution)/shard_map/ppermute | solution.py:282
  40.3 19.2 %collective-permute-start.21 = (bf16[96,768]{1,0:T(8,128)(2,1)}, bf16[96,768]{1,0:T(8,128)(2,1)S(1)}, u32[]{:S(2)}, u32[]{:S(2)}) collective-permute-start(bf16[96,768]{1,0:T(8,128)(2,1)} %param.29), channel_id=1, source_target_pairs={{0,16},{1,17},{2,18},{3,19},{4,20},{5,21},{6,22},{7,23},{8,24},{9,... | collective-permute-start | bytes 442376 | tf_op jit(solution)/shard_map/ppermute | solution.py:282
  45.9 15.1 %collective-permute-start.22 = (bf16[96,768]{1,0:T(8,128)(2,1)}, bf16[96,768]{1,0:T(8,128)(2,1)S(1)}, u32[]{:S(2)}, u32[]{:S(2)}) collective-permute-start(bf16[96,768]{1,0:T(8,128)(2,1)} %param.29), channel_id=1, source_target_pairs={{0,8},{1,9},{2,10},{3,11},{4,12},{5,13},{6,14},{7,15},{8,16},{9,17... | collective-permute-start | bytes 442376 | tf_op jit(solution)/shard_map/ppermute | solution.py:282
  49.2 60.4 %collective-permute-start = (bf16[1024,768]{0,1:T(8,128)(2,1)S(1)}, bf16[1024,768]{0,1:T(8,128)(2,1)}, u32[]{:S(2)}, u32[]{:S(2)}) collective-permute-start(bf16[1024,768]{0,1:T(8,128)(2,1)S(1)} %get-tuple-element.170), channel_id=1, source_target_pairs={{0,1},{1,0},{2,3},{3,2},{4,5},{5,4},{6,7},{7,6},{8,9},{9,8},{10,11... | collective-permute-start | bytes 4718600 | tf_op jit(solution)/shard_map/ppermute | solution.py:290
  49.2 15.1 %collective-permute-start.10 = (bf16[4,96,192]{1,2,0:T(8,128)(2,1)S(1)}, bf16[4,96,192]{1,2,0:T(8,128)(2,1)S(1)}, u32[]{:S(2)}, u32[]{:S(2)}) collective-permute-start(bf16[4,96,192]{1,2,0:T(8,128)(2,1)S(1)} %copy-done.44), channel_id=1, source_target_pairs={{0,2},{1,3},{2,0},{3,1},{4,6},{5,7},{6,4},{7,5},{8,10},{9,11},{10,... | collective-permute-start | bytes 442376 | tf_op jit(solution)/shard_map/ppermute | solution.py:290
  52.6 14.5 %collective-permute-start.4 = (bf16[4,96,576]{2,1,0:T(8,128)(2,1)}, bf16[4,96,576]{2,1,0:T(8,128)(2,1)}, u32[]{:S(2)}, u32[]{:S(2)}) collective-permute-start(bf16[4,96,576]{2,1,0:T(8,128)(2,1)} %copy.155), channel_id=1, source_target_pairs={{0,4},{1,5},{2,6},{3,7},{4,0},{5,1},{6,2},{7,3},{8,12},{9,13},{10,... | collective-permute-start | bytes 1327112 | tf_op jit(solution)/shard_map/ppermute | solution.py:282
  59.5 40.9 %collective-permute-start.17 = (bf16[4,96,768]{2,1,0:T(8,128)(2,1)}, bf16[4,96,768]{2,1,0:T(8,128)(2,1)}, u32[]{:S(2)}, u32[]{:S(2)}) collective-permute-start(bf16[4,96,768]{2,1,0:T(8,128)(2,1)} %constant_dynamic-slice_fusion.7), channel_id=1, source_target_pairs={{0,4},{1,5},{2,6},{3,7},{4,0},{5,1},{6,2},{7,3},{8,12},{9,13},{10,... | collective-permute-start | bytes 1769480 | tf_op jit(solution)/shard_map/ppermute | solution.py:282
  62.9 41.5 %collective-permute-start.23 = (bf16[4,96,768]{2,1,0:T(8,128)(2,1)}, bf16[4,96,768]{2,1,0:T(8,128)(2,1)}, u32[]{:S(2)}, u32[]{:S(2)}) collective-permute-start(bf16[4,96,768]{2,1,0:T(8,128)(2,1)} %constant_dynamic-slice_fusion.6), channel_id=1, source_target_pairs={{0,2},{1,3},{2,0},{3,1},{4,6},{5,7},{6,4},{7,5},{8,10},{9,11},{10,... | collective-permute-start | bytes 1769480 | tf_op jit(solution)/shard_map/ppermute | solution.py:290
  65.1 22.3 %collective-permute-start.11 = (bf16[2,4,96,192]{2,3,1,0:T(8,128)(2,1)}, bf16[2,4,96,192]{2,3,1,0:T(8,128)(2,1)}, u32[]{:S(2)}, u32[]{:S(2)}) collective-permute-start(bf16[2,4,96,192]{2,3,1,0:T(8,128)(2,1)} %pad_maximum_fusion.9), channel_id=1, source_target_pairs={{0,4},{1,5},{2,6},{3,7},{4,0},{5,1},{6,2},{7,3},{8,12},{9,13},{10,... | collective-permute-start | bytes 884744 | tf_op jit(solution)/shard_map/ppermute | solution.py:282
  73.9 34.2 %collective-permute-start.5 = (bf16[768,576]{0,1:T(8,128)(2,1)}, bf16[768,576]{0,1:T(8,128)(2,1)}, u32[]{:S(2)}, u32[]{:S(2)}) collective-permute-start(bf16[768,576]{0,1:T(8,128)(2,1)} %copy.160), channel_id=1, source_target_pairs={{0,2},{1,3},{2,0},{3,1},{4,6},{5,7},{6,4},{7,5},{8,10},{9,11},{10,... | collective-permute-start | bytes 2654216 | tf_op jit(solution)/shard_map/ppermute | solution.py:290
  94.0 84.3 %collective-permute-start.13 = (bf16[768,384]{0,1:T(8,128)(2,1)}, bf16[768,384]{0,1:T(8,128)(2,1)}, u32[]{:S(2)}, u32[]{:S(2)}) collective-permute-start(bf16[768,384]{0,1:T(8,128)(2,1)} %bitcast.302), channel_id=1, source_target_pairs={{0,1},{1,0},{2,3},{3,2},{4,5},{5,4},{6,7},{7,6},{8,9},{9,8},{10,11... | collective-permute-start | bytes 1769480 | tf_op jit(solution)/shard_map/ppermute | solution.py:290
  102.9 66.2 %collective-permute-start.18 = (bf16[768,768]{1,0:T(8,128)(2,1)}, bf16[768,768]{1,0:T(8,128)(2,1)}, u32[]{:S(2)}, u32[]{:S(2)}) collective-permute-start(bf16[768,768]{1,0:T(8,128)(2,1)} %bitcast.42), channel_id=1, source_target_pairs={{0,2},{1,3},{2,0},{3,1},{4,6},{5,7},{6,4},{7,5},{8,10},{9,11},{10,... | collective-permute-start | bytes 3538952 | tf_op jit(solution)/shard_map/ppermute | solution.py:290
  106.6 67.3 %collective-permute-start.24 = (bf16[2,4,96,768]{3,2,1,0:T(8,128)(2,1)}, bf16[2,4,96,768]{3,2,1,0:T(8,128)(2,1)}, u32[]{:S(2)}, u32[]{:S(2)}) collective-permute-start(bf16[2,4,96,768]{3,2,1,0:T(8,128)(2,1)} %pad_maximum_fusion.7), channel_id=1, source_target_pairs={{0,4},{1,5},{2,6},{3,7},{4,0},{5,1},{6,2},{7,3},{8,12},{9,13},{10,... | collective-permute-start | bytes 3538952 | tf_op jit(solution)/shard_map/ppermute | solution.py:282
  165.1 13.2 %collective-permute-start.12 = (bf16[1024,384]{1,0:T(8,128)(2,1)}, bf16[1024,384]{1,0:T(8,128)(2,1)}, u32[]{:S(2)}, u32[]{:S(2)}) collective-permute-start(bf16[1024,384]{1,0:T(8,128)(2,1)} %dynamic-slice_bitcast_fusion), channel_id=1, source_target_pairs={{0,1},{1,0},{2,3},{3,2},{4,5},{5,4},{6,7},{7,6},{8,9},{9,8},{10,11... | collective-permute-start | bytes 2359304 | tf_op jit(solution)/shard_map/ppermute | solution.py:290
  173.4 34.0 %collective-permute-start.25 = (bf16[768,1536]{0,1:T(8,128)(2,1)}, bf16[768,1536]{0,1:T(8,128)(2,1)}, u32[]{:S(2)}, u32[]{:S(2)}) collective-permute-start(bf16[768,1536]{0,1:T(8,128)(2,1)} %bitcast.305), channel_id=1, source_target_pairs={{0,1},{1,0},{2,3},{3,2},{4,5},{5,4},{6,7},{7,6},{8,9},{9,8},{10,11... | collective-permute-start | bytes 7077896 | tf_op jit(solution)/shard_map/ppermute | solution.py:290
  178.3 48.9 %collective-permute-start.26 = (bf16[768,1536]{0,1:T(8,128)(2,1)}, bf16[768,1536]{0,1:T(8,128)(2,1)S(1)}, u32[]{:S(2)}, u32[]{:S(2)}) collective-permute-start(bf16[768,1536]{0,1:T(8,128)(2,1)} %bitcast.308), channel_id=1, source_target_pairs={{0,1},{1,0},{2,3},{3,2},{4,5},{5,4},{6,7},{7,6},{8,9},{9,8},{10,11... | collective-permute-start | bytes 7077896 | tf_op jit(solution)/shard_map/ppermute | solution.py:290
  282.0 148.7 %collective-permute-start.45 = (bf16[768,1536]{1,0:T(8,128)(2,1)}, bf16[768,1536]{1,0:T(8,128)(2,1)}, u32[]{:S(2)}, u32[]{:S(2)}) collective-permute-start(bf16[768,1536]{1,0:T(8,128)(2,1)} %convolution_convert_fusion.1), channel_id=1, source_target_pairs={{0,1},{1,0},{2,3},{3,2},{4,5},{5,4},{6,7},{7,6},{8,9},{9,8},{10,11... | collective-permute-start | bytes 7077896 | tf_op jit(solution)/shard_map/ppermute | solution.py:290
  282.3 155.3 %collective-permute-start.51 = (bf16[768,1536]{1,0:T(8,128)(2,1)}, bf16[768,1536]{1,0:T(8,128)(2,1)}, u32[]{:S(2)}, u32[]{:S(2)}) collective-permute-start(bf16[768,1536]{1,0:T(8,128)(2,1)} %convolution_convert_fusion), channel_id=1, source_target_pairs={{0,1},{1,0},{2,3},{3,2},{4,5},{5,4},{6,7},{7,6},{8,9},{9,8},{10,11... | collective-permute-start | bytes 7077896 | tf_op jit(solution)/shard_map/ppermute | solution.py:290
  286.3 103.2 %collective-permute-start.40 = (bf16[768,192]{0,1:T(8,128)(2,1)}, bf16[768,192]{0,1:T(8,128)(2,1)}, u32[]{:S(2)}, u32[]{:S(2)}) collective-permute-start(bf16[768,192]{0,1:T(8,128)(2,1)} %fusion.36), channel_id=1, source_target_pairs={{0,2},{1,3},{2,0},{3,1},{4,6},{5,7},{6,4},{7,5},{8,10},{9,11},{10,... | collective-permute-start | bytes 884744 | tf_op jit(solution)/shard_map/ppermute | solution.py:290
  383.7 39.0 %collective-permute-start.28 = (bf16[1024,768]{0,1:T(8,128)(2,1)}, bf16[1024,768]{0,1:T(8,128)(2,1)}, u32[]{:S(2)}, u32[]{:S(2)}) collective-permute-start(bf16[1024,768]{0,1:T(8,128)(2,1)} %bitcast.240), channel_id=1, source_target_pairs={{0,1},{1,0},{2,3},{3,2},{4,5},{5,4},{6,7},{7,6},{8,9},{9,8},{10,11... | collective-permute-start | bytes 4718600 | tf_op jit(solution)/shard_map/ppermute | solution.py:290
  387.3 22.0 %collective-permute-start.34 = (bf16[768,576]{0,1:T(8,128)(2,1)}, bf16[768,576]{0,1:T(8,128)(2,1)}, u32[]{:S(2)}, u32[]{:S(2)}) collective-permute-start(bf16[768,576]{0,1:T(8,128)(2,1)} %bitcast.71), channel_id=1, source_target_pairs={{0,2},{1,3},{2,0},{3,1},{4,6},{5,7},{6,4},{7,5},{8,10},{9,11},{10,... | collective-permute-start | bytes 2654216 | tf_op jit(solution)/shard_map/ppermute | solution.py:290
  406.2 62.1 %collective-permute-start.44 = (bf16[96,192]{0,1:T(8,128)(2,1)S(1)}, bf16[96,192]{0,1:T(8,128)(2,1)S(1)}, u32[]{:S(2)}, u32[]{:S(2)}) collective-permute-start(bf16[96,192]{0,1:T(8,128)(2,1)S(1)} %get-tuple-element.154), channel_id=1, source_target_pairs={{0,24},{1,25},{2,26},{3,27},{4,28},{5,29},{6,30},{7,31},{8,0},{9,1... | collective-permute-start | bytes 110600 | tf_op jit(solution)/shard_map/ppermute | solution.py:282
  409.4 59.7 %collective-permute-start.43 = (bf16[96,192]{0,1:T(8,128)(2,1)S(1)}, bf16[96,192]{0,1:T(8,128)(2,1)S(1)}, u32[]{:S(2)}, u32[]{:S(2)}) collective-permute-start(bf16[96,192]{0,1:T(8,128)(2,1)S(1)} %get-tuple-element.155), channel_id=1, source_target_pairs={{0,16},{1,17},{2,18},{3,19},{4,20},{5,21},{6,22},{7,23},{8,24},{9,... | collective-permute-start | bytes 110600 | tf_op jit(solution)/shard_map/ppermute | solution.py:282
  422.7 29.3 %collective-permute-start.35 = (bf16[4,96,576]{2,1,0:T(8,128)(2,1)}, bf16[4,96,576]{2,1,0:T(8,128)(2,1)}, u32[]{:S(2)}, u32[]{:S(2)}) collective-permute-start(bf16[4,96,576]{2,1,0:T(8,128)(2,1)} %fusion.35), channel_id=1, source_target_pairs={{0,4},{1,5},{2,6},{3,7},{4,0},{5,1},{6,2},{7,3},{8,12},{9,13},{10,... | collective-permute-start | bytes 1327112 | tf_op jit(solution)/shard_map/ppermute | solution.py:282
  430.7 14.5 %collective-permute-start.29 = (f32[24576]{0:T(1024)S(1)}, f32[24576]{0:T(1024)S(1)}, u32[]{:S(2)}, u32[]{:S(2)}) collective-permute-start(f32[24576]{0:T(1024)S(1)} %constant_dynamic-update-slice_fusion.12), channel_id=1, source_target_pairs={{0,1},{1,0},{2,3},{3,2},{4,5},{5,4},{6,7},{7,6},{8,9},{9,8},{10,11... | collective-permute-start | bytes 294920 | tf_op jit(solution)/shard_map/ppermute | solution.py:290
  437.7 58.0 %collective-permute-start.46 = (bf16[2,4,96,768]{3,2,1,0:T(8,128)(2,1)}, bf16[2,4,96,768]{3,2,1,0:T(8,128)(2,1)}, u32[]{:S(2)}, u32[]{:S(2)}) collective-permute-start(bf16[2,4,96,768]{3,2,1,0:T(8,128)(2,1)} %fusion.21), channel_id=1, source_target_pairs={{0,4},{1,5},{2,6},{3,7},{4,0},{5,1},{6,2},{7,3},{8,12},{9,13},{10,... | collective-permute-start | bytes 3538952 | tf_op jit(solution)/shard_map/ppermute | solution.py:282
  450.5 49.9 %collective-permute-start.52 = (bf16[768,768]{1,0:T(8,128)(2,1)}, bf16[768,768]{1,0:T(8,128)(2,1)}, u32[]{:S(2)}, u32[]{:S(2)}) collective-permute-start(bf16[768,768]{1,0:T(8,128)(2,1)} %fusion.22), channel_id=1, source_target_pairs={{0,2},{1,3},{2,0},{3,1},{4,6},{5,7},{6,4},{7,5},{8,10},{9,11},{10,... | collective-permute-start | bytes 3538952 | tf_op jit(solution)/shard_map/ppermute | solution.py:290
  452.0 16.3 %collective-permute-start.31 = (f32[24576]{0:T(1024)S(1)}, f32[24576]{0:T(1024)S(1)}, u32[]{:S(2)}, u32[]{:S(2)}) collective-permute-start(f32[24576]{0:T(1024)S(1)} %add.403), channel_id=1, source_target_pairs={{0,4},{1,5},{2,6},{3,7},{4,0},{5,1},{6,2},{7,3},{8,12},{9,13},{10,... | collective-permute-start | bytes 294920 | tf_op jit(solution)/shard_map/ppermute | solution.py:286
  469.1 8.6 %collective-permute-start.38 = (bf16[96,576]{1,0:T(8,128)(2,1)S(1)}, bf16[96,576]{1,0:T(8,128)(2,1)S(1)}, u32[]{:S(2)}, u32[]{:S(2)}) collective-permute-start(bf16[96,576]{1,0:T(8,128)(2,1)S(1)} %get-tuple-element.149), channel_id=1, source_target_pairs={{0,24},{1,25},{2,26},{3,27},{4,28},{5,29},{6,30},{7,31},{8,0},{9,1... | collective-permute-start | bytes 331784 | tf_op jit(solution)/shard_map/ppermute | solution.py:282
  474.8 13.1 %collective-permute-start.37 = (bf16[96,576]{1,0:T(8,128)(2,1)S(1)}, bf16[96,576]{1,0:T(8,128)(2,1)S(1)}, u32[]{:S(2)}, u32[]{:S(2)}) collective-permute-start(bf16[96,576]{1,0:T(8,128)(2,1)S(1)} %get-tuple-element.150), channel_id=1, source_target_pairs={{0,16},{1,17},{2,18},{3,19},{4,20},{5,21},{6,22},{7,23},{8,24},{9,... | collective-permute-start | bytes 331784 | tf_op jit(solution)/shard_map/ppermute | solution.py:282
  475.2 12.7 %collective-permute-start.36 = (bf16[96,576]{1,0:T(8,128)(2,1)S(1)}, bf16[96,576]{1,0:T(8,128)(2,1)S(1)}, u32[]{:S(2)}, u32[]{:S(2)}) collective-permute-start(bf16[96,576]{1,0:T(8,128)(2,1)S(1)} %get-tuple-element.148), channel_id=1, source_target_pairs={{0,8},{1,9},{2,10},{3,11},{4,12},{5,13},{6,14},{7,15},{8,16},{9,17... | collective-permute-start | bytes 331784 | tf_op jit(solution)/shard_map/ppermute | solution.py:282
  477.7 17.0 %collective-permute-start.33 = (f32[24576]{0:T(1024)}, f32[24576]{0:T(1024)}, u32[]{:S(2)}, u32[]{:S(2)}) collective-permute-start(f32[24576]{0:T(1024)} %add.405), channel_id=1, source_target_pairs={{0,16},{1,17},{2,18},{3,19},{4,20},{5,21},{6,22},{7,23},{8,24},{9,... | collective-permute-start | bytes 294920 | tf_op jit(solution)/shard_map/ppermute | solution.py:286
  498.8 10.2 %collective-permute-start.47 = (bf16[4,96,768]{2,1,0:T(8,128)(2,1)}, bf16[4,96,768]{2,1,0:T(8,128)(2,1)}, u32[]{:S(2)}, u32[]{:S(2)}) collective-permute-start(bf16[4,96,768]{2,1,0:T(8,128)(2,1)} %fusion.33), channel_id=1, source_target_pairs={{0,2},{1,3},{2,0},{3,1},{4,6},{5,7},{6,4},{7,5},{8,10},{9,11},{10,... | collective-permute-start | bytes 1769480 | tf_op jit(solution)/shard_map/ppermute | solution.py:290
  504.0 13.9 %collective-permute-start.53 = (bf16[4,96,768]{2,1,0:T(8,128)(2,1)S(1)}, bf16[4,96,768]{2,1,0:T(8,128)(2,1)}, u32[]{:S(2)}, u32[]{:S(2)}) collective-permute-start(bf16[4,96,768]{2,1,0:T(8,128)(2,1)S(1)} %fusion.32), channel_id=1, source_target_pairs={{0,4},{1,5},{2,6},{3,7},{4,0},{5,1},{6,2},{7,3},{8,12},{9,13},{10,... | collective-permute-start | bytes 1769480 | tf_op jit(solution)/shard_map/ppermute | solution.py:282
  510.3 10.8 %collective-permute-start.50 = (bf16[96,768]{1,0:T(8,128)(2,1)S(1)}, bf16[96,768]{1,0:T(8,128)(2,1)S(1)}, u32[]{:S(2)}, u32[]{:S(2)}) collective-permute-start(bf16[96,768]{1,0:T(8,128)(2,1)S(1)} %get-tuple-element.142), channel_id=1, source_target_pairs={{0,24},{1,25},{2,26},{3,27},{4,28},{5,29},{6,30},{7,31},{8,0},{9,1... | collective-permute-start | bytes 442376 | tf_op jit(solution)/shard_map/ppermute | solution.py:282
  513.1 23.3 %collective-permute-start.49 = (bf16[96,768]{1,0:T(8,128)(2,1)S(1)}, bf16[96,768]{1,0:T(8,128)(2,1)S(1)}, u32[]{:S(2)}, u32[]{:S(2)}) collective-permute-start(bf16[96,768]{1,0:T(8,128)(2,1)S(1)} %get-tuple-element.143), channel_id=1, source_target_pairs={{0,16},{1,17},{2,18},{3,19},{4,20},{5,21},{6,22},{7,23},{8,24},{9,... | collective-permute-start | bytes 442376 | tf_op jit(solution)/shard_map/ppermute | solution.py:282
  516.0 20.4 %collective-permute-start.48 = (bf16[96,768]{1,0:T(8,128)(2,1)S(1)}, bf16[96,768]{1,0:T(8,128)(2,1)S(1)}, u32[]{:S(2)}, u32[]{:S(2)}) collective-permute-start(bf16[96,768]{1,0:T(8,128)(2,1)S(1)} %get-tuple-element.141), channel_id=1, source_target_pairs={{0,8},{1,9},{2,10},{3,11},{4,12},{5,13},{6,14},{7,15},{8,16},{9,17... | collective-permute-start | bytes 442376 | tf_op jit(solution)/shard_map/ppermute | solution.py:282
  519.2 18.0 %collective-permute-start.56 = (bf16[96,768]{1,0:T(8,128)(2,1)S(1)}, bf16[96,768]{1,0:T(8,128)(2,1)S(1)}, u32[]{:S(2)}, u32[]{:S(2)}) collective-permute-start(bf16[96,768]{1,0:T(8,128)(2,1)S(1)} %get-tuple-element.139), channel_id=1, source_target_pairs={{0,24},{1,25},{2,26},{3,27},{4,28},{5,29},{6,30},{7,31},{8,0},{9,1... | collective-permute-start | bytes 442376 | tf_op jit(solution)/shard_map/ppermute | solution.py:282
  521.1 20.0 %collective-permute-start.55 = (bf16[96,768]{1,0:T(8,128)(2,1)S(1)}, bf16[96,768]{1,0:T(8,128)(2,1)S(1)}, u32[]{:S(2)}, u32[]{:S(2)}) collective-permute-start(bf16[96,768]{1,0:T(8,128)(2,1)S(1)} %get-tuple-element.140), channel_id=1, source_target_pairs={{0,16},{1,17},{2,18},{3,19},{4,20},{5,21},{6,22},{7,23},{8,24},{9,... | collective-permute-start | bytes 442376 | tf_op jit(solution)/shard_map/ppermute | solution.py:282
  521.1 20.0 %collective-permute-start.54 = (bf16[96,768]{1,0:T(8,128)(2,1)S(1)}, bf16[96,768]{1,0:T(8,128)(2,1)S(1)}, u32[]{:S(2)}, u32[]{:S(2)}) collective-permute-start(bf16[96,768]{1,0:T(8,128)(2,1)S(1)} %get-tuple-element.138), channel_id=1, source_target_pairs={{0,8},{1,9},{2,10},{3,11},{4,12},{5,13},{6,14},{7,15},{8,16},{9,17... | collective-permute-start | bytes 442376 | tf_op jit(solution)/shard_map/ppermute | solution.py:282
  (84 other events, 725.8 us)

commit v2 on v1

--- a/solution.py
+++ b/solution.py
@@ -1,3 +1,5 @@
+import functools
+
 import jax
 import jax.numpy as jnp
 from jax import lax
@@ -122,8 +124,8 @@
     )(first, last, q, k, v, kseg, qseg)
 
 
-def backward_kernel(first_ref, last_ref, q_ref, do_ref, k_ref, v_ref, kseg_ref, qseg_ref, lse_ref,
-                    dq_ref, dk_ref, dv_ref, kt_ref, qm_ref, dom_ref, p_ref, g_ref, delta_ref, dqt_ref, dka_ref, dva_ref):
+def backward_kernel(base, first_ref, last_ref, q_ref, do_ref, k_ref, v_ref, kseg_ref, qseg_ref, lse_ref,
+                    d_ref, kt_ref, qm_ref, dom_ref, p_ref, g_ref, delta_ref, dqt_ref, dka_ref, dva_ref):
     i = pl.program_id(0)
     tiles = pl.num_programs(0)
     pairs = q_ref.shape[1] // 128
@@ -163,7 +165,7 @@
                 part = None
                 for h in (2 * g, 2 * g + 1):
                     s = mm(kp, qm_ref[h], NT)
-                    p = jnp.where(seen, jnp.exp(s - lse_ref[h:h + 1, :]), 0.0)
+                    p = jnp.where(seen, jnp.exp(s - lse_ref[base + h:base + h + 1, :]), 0.0)
                     d = mm(vp, dom_ref[h], NT)
                     p_ref[h, t] = p
                     g_ref[h, t] = d
@@ -193,16 +195,17 @@
     lax.fori_loop(0, tiles, second_pass, 0)
     for g in range(pairs):
         pair = jnp.concatenate([dqt_ref[2 * g], dqt_ref[2 * g + 1]], axis=0)
-        dq_ref[:, 128 * g:128 * g + 128] = (pair.T * 0.125).astype(jnp.bfloat16)
+        own = pl.ds(pl.multiple_of(i * TILE, TILE), TILE)
+        d_ref[own, 128 * g:128 * g + 128] = (pair.T * 0.125).astype(jnp.bfloat16)
 
     @pl.when(i == tiles - 1)
     def _():
-        dk_ref[...] = dka_ref[...].astype(jnp.bfloat16)
-        dv_ref[...] = dva_ref[...].astype(jnp.bfloat16)
-
-
-def attend_backward(q, k, v, do, lse, seg):
-    n, width = q.shape
+        d_ref[:, 128 * pairs:256 * pairs] = dka_ref[...].astype(jnp.bfloat16)
+        d_ref[:, 256 * pairs:384 * pairs] = dva_ref[...].astype(jnp.bfloat16)
+
+
+def attend_backward(g, q, k, v, do, lse, seg):
+    n, width = q.shape[0], 128
     tiles = n // TILE
     heads = width // 64
     first = seg[::TILE]
@@ -210,16 +213,16 @@
     kseg = jnp.broadcast_to(seg[:, None], (n, 128))
     qseg = jnp.broadcast_to(seg[None, :], (8, n))
     whole = lambda shape: pl.BlockSpec(shape, lambda i, *_: (0,) * len(shape))
-    rows = pl.BlockSpec((TILE, width), lambda i, *_: (i, 0))
+    rows = pl.BlockSpec((TILE, width), lambda i, *_: (i, g))
+    column = pl.BlockSpec((n, width), lambda i, *_: (0, g))
     stat = pl.BlockSpec((8, TILE), lambda i, *_: (0, i))
-    out = jax.ShapeDtypeStruct((n, width), jnp.bfloat16)
     return pl.pallas_call(
-        backward_kernel,
-        out_shape=(out, out, out),
+        functools.partial(backward_kernel, 2 * g),
+        out_shape=jax.ShapeDtypeStruct((n, 3 * width), jnp.bfloat16),
         grid_spec=pltpu.PrefetchScalarGridSpec(
             num_scalar_prefetch=2, grid=(tiles,),
-            in_specs=[rows, rows, whole((n, width)), whole((n, width)), whole((n, 128)), stat, stat],
-            out_specs=[rows, whole((n, width)), whole((n, width))],
+            in_specs=[rows, rows, column, column, whole((n, 128)), stat, stat],
+            out_specs=whole((n, 3 * width)),
             scratch_shapes=[
                 pltpu.VMEM((tiles, width, TILE), jnp.bfloat16),
                 pltpu.VMEM((heads, TILE, 128), jnp.bfloat16),
@@ -237,6 +240,487 @@
     )(first, last, q, do, k, v, kseg, qseg, lse)
 
 
+BLOCK = 256
+STRIP = 64
+
+
+def normal_cdf_parts(u):
+    v = u * 0.7071067811865476
+    c = jnp.clip(v, -3.832506856900711, 3.832506856900711)
+    c2 = c * c
+    top = 0.00022905065861350646
+    for a in (0.0034082910107109506, 0.050955695062380861, 0.18520832239976145, 1.128379143519084):
+        top = top * c2 + a
+    low = -1.1791602954361697e-7
+    for b in (0.000023547966471313185, 0.0010179625278914885, 0.014070470171167667, 0.11098505178285362,
+              0.49746925110067538, 1.0):
+        low = low * c2 + b
+    cdf = 0.5 + 0.5 * (c * top / low)
+    slope = jnp.exp(-(v * v)) * (u * 0.3989422804014327)
+    return u * cdf, cdf + slope
+
+
+def middle_kernel(pieces, o_all, x0, outs, ups, downs, cot, vec_ref, bup_ref,
+                  block_out, dr1, do_all, g_down, g_up, g_out, sums_ref, upsum_ref,
+                  o_ref, raw_ref, wo_ref, wu_ref, wd_ref, hat_ref, inv_ref, acc_ref, hl_ref, hlt_ref, gp_ref, z_ref, c_ref,
+                  df_ref, dft_ref, y_ref, st_ref, su_ref, ru_ref, rd_ref, go_ref, rgo_ref, u0_ref, u1_ref,
+                  sem, osem, send, recv):
+    f32, bf16 = jnp.float32, jnp.bfloat16
+    rows, width = hat_ref.shape
+    blocks = rows // BLOCK
+    part = wu_ref.shape[2]
+    bf = lambda a: a.astype(bf16)
+    dp, tensor = lax.axis_index("dp"), lax.axis_index("tensor")
+    inner = tensor % 2
+    partner = (dp, tensor + 1 - 2 * inner)
+    mine = pl.multiple_of(inner * rows, 1024)
+    theirs = pl.multiple_of((1 - inner) * rows, 1024)
+    greet([partner])
+
+    def remote(n, src, dst):
+        return pltpu.make_async_remote_copy(src, dst, send.at[n], recv.at[n], device_id=partner,
+                                            device_id_type=pl.DeviceIdType.MESH)
+
+    swap_o = remote(0, o_all.at[pl.ds(theirs, rows), :], o_ref.at[1])
+    swap_o.start()
+    count = [0]
+
+    def load(src, dst):
+        copy = pltpu.make_async_copy(src, dst, sem.at[count[0]])
+        count[0] += 1
+        copy.start()
+        return copy
+
+    def weight(sources, dst):
+        if not pieces:
+            return [load(sources[0].at[o], dst.at[o]) for o in range(2)]
+        digit = dp % 2
+        made = []
+        for o in range(2):
+            for zi in range(sources[0].shape[1]):
+                for n in range(2):
+                    place = 2 * zi + (digit if n == 0 else 1 - digit)
+                    r = sources[n].shape[2]
+                    made.append(load(sources[n].at[o, zi], dst.at[o, pl.ds(pl.multiple_of(place * r, r), r), :]))
+        return made
+
+    first = [load(o_all.at[pl.ds(mine, rows), :], o_ref.at[0]), load(x0, hat_ref)] + weight(outs, raw_ref.at[0])
+    if pieces:
+        second = [load(ups[o], wu_ref.at[o]) for o in range(2)]
+    else:
+        second = [load(ups[0].at[o], wu_ref.at[o]) for o in range(2)]
+    second = second + weight(downs, wd_ref)
+    late = load(cot, c_ref)
+    vec = lambda n: vec_ref[n:n + 1, :]
+    sums_ref[...] = jnp.zeros_like(sums_ref)
+    upsum_ref[...] = jnp.zeros_like(upsum_ref)
+    for copy in first:
+        copy.wait()
+    swaps = [remote(1, raw_ref.at[0], raw_ref.at[1])]
+    swaps[0].start()
+    for copy in second:
+        copy.wait()
+    for o in range(2):
+        swaps.append(remote(2 + 2 * o, wu_ref.at[o], wu_ref.at[2 + o]))
+        swaps.append(remote(3 + 2 * o, wd_ref.at[o], wd_ref.at[2 + o]))
+    for copy in swaps[1:]:
+        copy.start()
+    lane = lax.broadcasted_iota(jnp.int32, (width, 128), 1)
+
+    def order_heads(side):
+        wo_ref[side, :, 0:128] = raw_ref[side, 0, :, 0:128]
+        wo_ref[side, :, 128:256] = raw_ref[side, 1, :, 0:128]
+        upper = pltpu.roll(raw_ref[side, 1, :, 128:256].astype(f32), 64, 1)
+        wo_ref[side, :, 256:384] = bf(jnp.where(lane < 64, raw_ref[side, 0, :, 128:256].astype(f32), upper))
+    order_heads(0)
+    swaps[0].wait()
+    order_heads(1)
+    swap_o.wait()
+
+    def strips(body):
+        def run(s, carry):
+            body(pl.ds(pl.multiple_of(s * STRIP, STRIP), STRIP))
+            return carry
+        lax.fori_loop(0, rows // STRIP, run, 0)
+
+    def add_sum(n, value):
+        sums_ref[n] = sums_ref[n] + jnp.sum(fold(value), axis=0)
+
+    def fold(value):
+        return value.reshape(value.shape[0] // 8, 8, value.shape[1])
+
+    def mean(value):
+        return jnp.sum(value, axis=-1, keepdims=True) * (1.0 / width)
+
+    def project(b, carry):
+        r = pl.ds(pl.multiple_of(b * BLOCK, BLOCK), BLOCK)
+        acc_ref[r, :] = mm(o_ref[0, r, :], wo_ref[0], NT) + mm(o_ref[1, r, :], wo_ref[1], NT)
+        return carry
+    lax.fori_loop(0, blocks, project, 0)
+
+    def first_norm(r):
+        r1 = hat_ref[r, :] + (acc_ref[r, :] + vec(0))
+        centre = r1 - mean(r1)
+        inv = lax.rsqrt(mean(centre * centre) + EPSILON)
+        hat = centre * inv
+        hat_ref[r, :] = hat
+        inv_ref[r, :] = inv
+        hl_ref[r, :] = bf(hat * vec(1) + vec(2))
+    strips(first_norm)
+    for b in range(blocks):
+        hlt_ref[:, BLOCK * b:BLOCK * b + BLOCK] = hl_ref[BLOCK * b:BLOCK * b + BLOCK, :].T
+    acc_ref[...] = jnp.zeros_like(acc_ref)
+
+    bufs = (u0_ref, u1_ref)
+
+    def forward(j, carry):
+        for o in range(2):
+            @pl.when(j == 2 + o)
+            def _(o=o):
+                swaps[1 + 2 * o].wait()
+                swaps[2 + 2 * o].wait()
+
+        def lift(b):
+            bufs[b % 2][...] = mm(hl_ref[BLOCK * b:BLOCK * b + BLOCK, :], wu_ref[j]) + bup_ref[j]
+        lift(0)
+        for b in range(blocks):
+            if b + 1 < blocks:
+                lift(b + 1)
+            r = slice(BLOCK * b, BLOCK * b + BLOCK)
+            for i in range(0, BLOCK, 32):
+                for w in range(0, part, 256):
+                    z, gp = normal_cdf_parts(bufs[b % 2][i:i + 32, w:w + 256])
+                    z_ref[j, BLOCK * b + i:BLOCK * b + i + 32, w:w + 256] = bf(z)
+                    gp_ref[j, BLOCK * b + i:BLOCK * b + i + 32, w:w + 256] = gp
+            acc_ref[r, :] = acc_ref[r, :] + mm(z_ref[j, r, :], wd_ref[j], NT)
+        return carry
+    lax.fori_loop(0, 4, forward, 0)
+    late.wait()
+
+    def second_norm(r):
+        h1 = hat_ref[r, :] * vec(1) + vec(2)
+        r2 = h1 + (acc_ref[r, :] + vec(3))
+        centre = r2 - mean(r2)
+        inv = lax.rsqrt(mean(centre * centre) + EPSILON)
+        hat = centre * inv
+        y_ref[r, :] = bf(hat * vec(4) + vec(5))
+        c = c_ref[r, :].astype(f32)
+        add_sum(0, c * hat)
+        add_sum(1, c)
+        w = c * vec(4)
+        dr2 = (w - mean(w) - hat * mean(w * hat)) * inv
+        acc_ref[r, :] = dr2
+        low = bf(dr2)
+        df_ref[r, :] = low
+        add_sum(2, low.astype(f32))
+    strips(second_norm)
+    stores = [pltpu.make_async_copy(y_ref, block_out, osem.at[0])]
+    stores[0].start()
+    for b in range(blocks):
+        dft_ref[:, BLOCK * b:BLOCK * b + BLOCK] = df_ref[BLOCK * b:BLOCK * b + BLOCK, :].T
+
+    def backward(n, carry):
+        j = 3 - n
+
+        def lower(b):
+            bufs[b % 2][...] = mm(df_ref[BLOCK * b:BLOCK * b + BLOCK, :], wd_ref[j])
+        slot = n % 2
+        away = [remote(6 + slot, st_ref.at[slot], rd_ref.at[slot]), remote(8 + slot, su_ref.at[slot], ru_ref.at[slot])]
+        lower(0)
+        for b in range(blocks):
+            if b + 1 < blocks:
+                lower(b + 1)
+            r = slice(BLOCK * b, BLOCK * b + BLOCK)
+            for i in range(0, BLOCK, 64):
+                q = slice(BLOCK * b + i, BLOCK * b + i + 64)
+                dul = bf(bufs[b % 2][i:i + 64, :] * gp_ref[j, q, :])
+                upsum_ref[j] = upsum_ref[j] + jnp.sum(fold(dul.astype(f32)), axis=0)
+                hat2_ref[q, :] = dul
+            acc_ref[r, :] = acc_ref[r, :] + mm(hat2_ref[r, :], wu_ref[j], NT)
+
+        @pl.when(n < 2)
+        def _():
+            for m in range(0, width, BLOCK):
+                st_ref[slot, m:m + BLOCK, :] = bf(mm(dft_ref[m:m + BLOCK, :], z_ref[j]))
+            away[0].start()
+            for m in range(0, width, BLOCK):
+                su_ref[slot, m:m + BLOCK, :] = bf(mm(hlt_ref[m:m + BLOCK, :], hat2_ref[...]))
+            away[1].start()
+
+        @pl.when(n >= 2)
+        def _():
+            away[0].wait()
+            for m in range(0, width, BLOCK):
+                got = rd_ref[slot, m:m + BLOCK, :].astype(f32)
+                st_ref[slot, m:m + BLOCK, :] = bf(mm(dft_ref[m:m + BLOCK, :], z_ref[j]) + got)
+            pltpu.make_async_copy(st_ref.at[slot], g_down.at[j], osem.at[1 + slot]).start()
+            away[1].wait()
+            for m in range(0, width, BLOCK):
+                got = ru_ref[slot, m:m + BLOCK, :].astype(f32)
+                su_ref[slot, m:m + BLOCK, :] = bf(mm(hlt_ref[m:m + BLOCK, :], hat2_ref[...]) + got)
+            pltpu.make_async_copy(su_ref.at[slot], g_up.at[j], osem.at[3 + slot]).start()
+        return carry
+    hat2_ref = y_ref
+    stores[0].wait()
+    lax.fori_loop(0, 4, backward, 0)
+
+    def first_back(r):
+        dh1 = acc_ref[r, :]
+        hat = hat_ref[r, :]
+        add_sum(3, dh1 * hat)
+        add_sum(4, dh1)
+        w = dh1 * vec(1)
+        grad = (w - mean(w) - hat * mean(w * hat)) * inv_ref[r, :]
+        acc_ref[r, :] = grad
+        low = bf(grad)
+        df_ref[r, :] = low
+        add_sum(5, low.astype(f32))
+    strips(first_back)
+    out = pltpu.make_async_copy(acc_ref, dr1, osem.at[0])
+    out.start()
+    stores = [out]
+    for b in range(blocks):
+        dft_ref[:, BLOCK * b:BLOCK * b + BLOCK] = df_ref[BLOCK * b:BLOCK * b + BLOCK, :].T
+    lane = lax.broadcasted_iota(jnp.int32, (BLOCK, 128), 1)
+
+    def out_grad(side, m):
+        tiles = [mm(dft_ref[m:m + BLOCK, :], o_ref[side, :, 128 * g:128 * g + 128]) for g in range(3)]
+        third = [jnp.where(lane < 64, tiles[2], 0.0), jnp.where(lane < 64, pltpu.roll(tiles[2], 64, 1), 0.0)]
+        return [jnp.concatenate([tiles[o], third[o]], axis=1) for o in range(2)]
+    for m in range(0, width, BLOCK):
+        for o, value in enumerate(out_grad(1, m)):
+            go_ref[o, m:m + BLOCK, :] = bf(value)
+    swap_go = remote(10, go_ref, rgo_ref)
+    swap_go.start()
+    ow = wo_ref.shape[2]
+    for side in (1, 0):
+        def push(b, carry):
+            r = pl.ds(pl.multiple_of(b * BLOCK, BLOCK), BLOCK)
+            y_ref[r, ow * side:ow * side + ow] = bf(mm(df_ref[r, :], wo_ref[side]))
+            return carry
+        lax.fori_loop(0, blocks, push, 0)
+        if side == 1:
+            swap_do = remote(11, y_ref.at[:, pl.ds(ow, ow)], do_all.at[pl.ds(mine, rows), :])
+            swap_do.start()
+        else:
+            copy = pltpu.make_async_copy(y_ref.at[:, pl.ds(0, ow)], do_all.at[pl.ds(mine, rows), :], osem.at[5])
+            copy.start()
+            stores.append(copy)
+    swap_go.wait()
+    for m in range(0, width, BLOCK):
+        for o, value in enumerate(out_grad(0, m)):
+            go_ref[o, m:m + BLOCK, :] = bf(value + rgo_ref[o, m:m + BLOCK, :].astype(f32))
+    copy = pltpu.make_async_copy(go_ref, g_out, osem.at[6])
+    copy.start()
+    stores.append(copy)
+    for slot in range(2):
+        pltpu.make_async_copy(st_ref.at[slot], g_down.at[0], osem.at[1 + slot]).wait()
+        pltpu.make_async_copy(su_ref.at[slot], g_up.at[0], osem.at[3 + slot]).wait()
+    swap_do.wait()
+    for copy in stores:
+        copy.wait()
+
+
+def middle(o_all, x0, outs, ups, downs, cot, vec, bup):
+    f32, bf16 = jnp.float32, jnp.bfloat16
+    rows, width = x0.shape
+    ow = o_all.shape[1]
+    part = bup.shape[-1]
+    pieces = len(ups) == 2
+    shape = jax.ShapeDtypeStruct
+    hbm = pl.BlockSpec(memory_space=pl.ANY)
+    vmem = pl.BlockSpec(memory_space=pltpu.VMEM)
+    v = pltpu.VMEM
+    n = len(ups)
+
+    def kernel(o_all, x0, *refs):
+        weights = refs[:3 * n]
+        middle_kernel(pieces, o_all, x0, weights[:n], weights[n:2 * n], weights[2 * n:], *refs[3 * n:])
+
+    return pl.pallas_call(
+        kernel,
+        out_shape=(shape((rows, width), bf16), shape((rows, width), f32), shape((2 * rows, ow), bf16),
+                   shape((2, width, part), bf16), shape((2, width, part), bf16), shape((2, width, 256), bf16),
+                   shape((6, 8, width), f32), shape((4, 8, part), f32)),
+        in_specs=[hbm] * (3 + 3 * n) + [vmem] * 2,
+        out_specs=[hbm] * 6 + [vmem] * 2,
+        scratch_shapes=[
+            v((2, rows, ow), bf16), v((2, 2, width, 256), bf16), v((2, width, ow), bf16), v((4, width, part), bf16),
+            v((4, width, part), bf16),
+            v((rows, width), f32), v((rows, 1), f32), v((rows, width), f32), v((rows, width), bf16), v((width, rows), bf16),
+            v((4, rows, part), f32), v((4, rows, part), bf16), v((rows, width), bf16), v((rows, width), bf16),
+            v((width, rows), bf16), v((rows, width), bf16), v((2, width, part), bf16),
+            v((2, width, part), bf16), v((2, width, part), bf16), v((2, width, part), bf16), v((2, width, 256), bf16),
+            v((2, width, 256), bf16), v((BLOCK, part), f32), v((BLOCK, part), f32),
+            pltpu.SemaphoreType.DMA((40,)), pltpu.SemaphoreType.DMA((7,)),
+            pltpu.SemaphoreType.DMA((12,)), pltpu.SemaphoreType.DMA((12,)),
+        ],
+        compiler_params=pltpu.CompilerParams(vmem_limit_bytes=VMEM_MAX, collective_id=1, has_side_effects=True),
+        cost_estimate=pl.CostEstimate(flops=6 * rows * width * 9 * width, bytes_accessed=60_000_000, transcendentals=2 * rows * 4 * part),
+        name="middle",
+    )(o_all, x0, *outs, *ups, *downs, cot, vec, bup)
+
+
+class Exchange:
+    def __init__(self, send, recv):
+        self.send, self.recv, self.used = send, recv, 0
+
+    def copy(self, src, dst, device):
+        n = self.used
+        self.used += 1
+        return pltpu.make_async_remote_copy(src, dst, self.send.at[n], self.recv.at[n], device_id=device,
+                                            device_id_type=pl.DeviceIdType.MESH)
+
+
+def greet(devices):
+    barrier = pltpu.get_barrier_semaphore()
+    for device in devices:
+        pl.semaphore_signal(barrier, inc=1, device_id=device, device_id_type=pl.DeviceIdType.MESH)
+    pl.semaphore_wait(barrier, len(devices))
+
+
+def entry_kernel(tokens, pos_ref, mem_ref, wq_ref, bq_ref, wu_ref, wd_ref, wo_ref,
+                 x0_out, x_out, q_out, k_out, v_out, w_out, up_g, down_g, out_g,
+                 x0_ref, x_ref, g_ref, b_ref, y_ref, q_ref, k_ref, v_ref, send, recv, sem):
+    f32, bf16 = jnp.float32, jnp.bfloat16
+    rows, width = x0_ref.shape
+    dp, tensor = lax.axis_index("dp"), lax.axis_index("tensor")
+    z, x = dp // 2, dp % 2
+    inner = tensor % 2
+    zs = [(z + 4 - k) % 4 for k in range(4)]
+    at = [2 * zs[k] + x for k in range(4)]
+    far = [2 * zs[k] + 1 - x for k in range(4)]
+    to_z = [None] + [(2 * ((z + k) % 4) + x, tensor) for k in range(1, 4)]
+    to_x = (2 * z + 1 - x, tensor)
+    to_y = (dp, (tensor + 2) % 4)
+    to_core = (dp, tensor + 1 - 2 * inner)
+    greet(to_z[1:] + [to_x, to_y, to_core])
+    ex = Exchange(send, recv)
+    started = []
+
+    def go(src, dst, device):
+        copy = ex.copy(src, dst, device)
+        copy.start()
+        started.append(copy)
+        return copy
+
+    local = []
+
+    def keep(src, dst):
+        copy = pltpu.make_async_copy(src, dst, sem.at[len(local)])
+        copy.start()
+        local.append(copy)
+        return copy
+
+    own = keep(wq_ref, g_ref.at[0, at[0]])
+    own_bias = keep(bq_ref, b_ref.at[0])
+    z_q = [None] + [go(wq_ref, g_ref.at[0, at[0]], to_z[k]) for k in range(1, 4)]
+    x_q = [go(wq_ref, g_ref.at[0, at[0]], to_x)]
+    y_q = [go(wq_ref, g_ref.at[1, at[0]], to_y)]
+    bias = go(bq_ref, b_ref.at[1], to_y)
+
+    mine = pl.multiple_of(inner * rows, 1024)
+    positions = pos_ref[0:1, :]
+    strip = 128
+
+    def start(s, carry):
+        r = pl.multiple_of(s * strip, strip)
+        place = lax.broadcasted_iota(jnp.int32, (strip, positions.shape[1]), 0) + (inner * rows + r)
+        picks = jnp.where(place == positions, 1.0, 0.0).astype(bf16)
+        value = tokens[pl.ds(r, strip), :].astype(f32) + mm(picks, mem_ref[...])
+        x0_ref[pl.ds(r, strip), :] = value
+        x_ref[pl.ds(mine + r, strip), :] = value.astype(bf16)
+        return carry
+    lax.fori_loop(0, rows // strip, start, 0)
+    keep(x0_ref, x0_out)
+    core = go(x_ref.at[pl.ds(mine, rows), :], x_ref.at[pl.ds(mine, rows), :], to_core)
+
+    for k in range(1, 4):
+        z_q[k].wait_recv()
+        x_q.append(go(g_ref.at[0, at[k]], g_ref.at[0, at[k]], to_x))
+        y_q.append(go(g_ref.at[0, at[k]], g_ref.at[1, at[k]], to_y))
+    z_u = [None] + [go(wu_ref, up_g.at[at[0]], to_z[k]) for k in range(1, 4)]
+    z_d = [None] + [go(wd_ref, down_g.at[0, z], to_z[k]) for k in range(1, 4)]
+    z_o = [None] + [go(wo_ref, out_g.at[0, z], to_z[k]) for k in range(1, 4)]
+    keep(wu_ref, up_g.at[at[0]])
+    keep(wd_ref, down_g.at[0, z])
+    keep(wo_ref, out_g.at[0, z])
+    last = []
+    for k in range(2):
+        x_q[k].wait_recv()
+        last.append(go(g_ref.at[0, far[k]], g_ref.at[1, far[k]], to_y))
+    for k in range(2, 4):
+        y_q[k].wait_recv()
+        last.append(go(g_ref.at[1, at[k]], g_ref.at[1, at[k]], to_x))
+    rest = [go(wu_ref, up_g.at[at[0]], to_x), go(wd_ref, down_g.at[1, z], to_y), go(wo_ref, out_g.at[1, z], to_y)]
+    for copy in x_q[2:] + y_q[:2] + last + [bias, core]:
+        copy.wait_recv()
+    own.wait()
+    own_bias.wait()
+    keep(g_ref, w_out)
+    keep(x_ref, x_out)
+
+    lane = lax.broadcasted_iota(jnp.int32, (BLOCK, 128), 1)
+    y_ref[...] = jnp.zeros_like(y_ref)
+
+    def project(b, carry):
+        r = pl.ds(pl.multiple_of(b * BLOCK, BLOCK), BLOCK)
+        for o in range(2):
+            y_ref[o, :, 0:576] = mm(x_ref[r, :], g_ref[o].reshape(width, 576)) + b_ref[o, 0:1, 0:576].astype(f32)
+        tile = lambda o, n: y_ref[o, :, 128 * n:128 * n + 128]
+        turn = lambda value: pltpu.roll(value, 64, 1)
+        third = (jnp.where(lane < 64, tile(0, 3), turn(tile(1, 3))), jnp.where(lane < 64, turn(tile(0, 3)), tile(1, 3)),
+                 jnp.where(lane < 64, tile(0, 4), turn(tile(1, 4))))
+        for n, ref in enumerate((q_ref, k_ref, v_ref)):
+            for g, value in enumerate((tile(0, n), tile(1, n), third[n])):
+                value = value.astype(bf16)
+                if n == 0:
+                    value = value * jnp.asarray(0.125, bf16)
+                ref[r, 128 * g:128 * g + 128] = value
+        return carry
+    lax.fori_loop(0, 2 * rows // BLOCK, project, 0)
+    for src, dst in ((q_ref, q_out), (k_ref, k_out), (v_ref, v_out)):
+        keep(src, dst)
+    for k in range(1, 4):
+        z_u[k].wait_recv()
+        rest.append(go(up_g.at[at[k]], up_g.at[at[k]], to_x))
+        z_d[k].wait_recv()
+        rest.append(go(down_g.at[0, zs[k]], down_g.at[1, zs[k]], to_y))
+        z_o[k].wait_recv()
+        rest.append(go(out_g.at[0, zs[k]], out_g.at[1, zs[k]], to_y))
+    for copy in rest:
+        copy.wait_recv()
+    for copy in started:
+        copy.wait_send()
+    for copy in local[2:]:
+        copy.wait()
+
+
+def entry(tokens, positions, memory_rows, shard_qkv, biases, up, down, out):
+    f32, bf16 = jnp.float32, jnp.bfloat16
+    rows, width = tokens.shape
+    r = up.shape[0]
+    shape, v = jax.ShapeDtypeStruct, pltpu.VMEM
+    hbm, vmem = pl.BlockSpec(memory_space=pl.ANY), pl.BlockSpec(memory_space=pltpu.VMEM)
+    qkv = shape((2 * rows, 384), bf16)
+    return pl.pallas_call(
+        entry_kernel,
+        out_shape=(shape((rows, width), f32), shape((2 * rows, width), bf16), qkv, qkv, qkv,
+                   shape((2, 8, r, 576), bf16), shape((8, r, up.shape[1]), bf16), shape((2, 4, r, down.shape[1]), bf16),
+                   shape((2, 4, r, out.shape[1]), bf16)),
+        in_specs=[vmem] * 8,
+        out_specs=[hbm] * 9,
+        scratch_shapes=[
+            v((rows, width), f32), v((2 * rows, width), bf16), v((2, 8, r, 576), bf16), v((2, 16, 640), bf16),
+            v((2, BLOCK, 640), f32), v((2 * rows, 384), bf16), v((2 * rows, 384), bf16), v((2 * rows, 384), bf16),
+            pltpu.SemaphoreType.DMA((48,)), pltpu.SemaphoreType.DMA((48,)), pltpu.SemaphoreType.DMA((16,)),
+        ],
+        compiler_params=pltpu.CompilerParams(vmem_limit_bytes=VMEM_MAX, collective_id=0, has_side_effects=True),
+        cost_estimate=pl.CostEstimate(flops=4 * rows * width * 1152, bytes_accessed=20_000_000, transcendentals=0),
+        name="entry",
+    )(tokens, positions, memory_rows, shard_qkv, biases, up, down, out)
+
+
 def layer_norm(values, norm_gain, norm_shift):
     centre = values - jnp.mean(values, axis=-1, keepdims=True)
     spread = jnp.mean(centre * centre, axis=-1, keepdims=True)
@@ -338,6 +822,23 @@
             value = self.reduce_stage(value, j, j)
         return value
 
+    @property
+    def stages(self):
+        return len(self.factors) + 1
+
+    def open(self, parts, outer_first):
+        columns = parts.shape[-1]
+        return parts if outer_first else parts.reshape(2, *self.factors, -1, columns)
+
+    def stage(self, value, outer_first, n):
+        count = len(self.factors)
+        if n == (0 if outer_first else 1):
+            value = value[0].astype(jnp.float32) + self.swap(value[1].astype(jnp.bfloat16), 2).astype(jnp.float32)
+            return value.reshape(*self.factors, -1, value.shape[-1]) if outer_first else value
+        if n == 0:
+            return self.reduce_stage(value, count - 1, count)
+        return self.reduce_stage(value, count - n, count - n)
+
     def total(self, vector):
         for bit in (1, 2):
             vector = vector + self.swap(vector, bit)
@@ -365,101 +866,91 @@
     positions = lax.dynamic_index_in_dim(memory_positions, outer, 0, keepdims=False)
     row_place = inner * rows + jnp.arange(rows, dtype=jnp.int32)
     picks = (row_place[:, None] == positions[None, :])
-    x0 = tokens.astype(f32) + jnp.dot(picks.astype(bf16), memory_rows, preferred_element_type=f32)
-    xl = x0.astype(bf16)
-
-    shard_qkv = qkv_weight.reshape(slice_rows, heads, 3, hd).transpose(0, 2, 1, 3).reshape(slice_rows, 3 * hw)
-    w_qkv = grid.gather(shard_qkv)
-    w_qkv = w_qkv.reshape(2, width, 3, hw).transpose(1, 2, 0, 3).reshape(width, 6 * hw)
-    other = grid.swap(xl, 1)
-    x_all = jnp.concatenate([jnp.where(inner == 0, xl, other), jnp.where(inner == 0, other, xl)])
-    w_out = grid.gather(out_weight.reshape(slice_rows, hw), True)
-    w_up = grid.gather(up_weight)
-    w_down = grid.gather(down_weight, True)
-
-    small = jnp.concatenate([qv_bias.reshape(-1), up_bias])
-    small_other = grid.swap(small, 2)
-    qv = jnp.stack([small[:2 * hw], small_other[:2 * hw]]).reshape(2, heads, 2, hd).astype(f32)
-    b_up = jnp.concatenate([small[2 * hw:], small_other[2 * hw:]])
+    joined = lambda w: w.transpose(1, 0, 2).reshape(width, -1)
+
+    parts = qkv_weight.reshape(slice_rows, heads, 3, hd)
+    order_columns = lambda p: jnp.concatenate([p[..., :2, n, :].reshape(*p.shape[:-3], 2 * hd) for n in range(3)]
+                                              + [p[..., 2, n, :] for n in range(3)], axis=-1)
+    shard_qkv = order_columns(parts)
+    shard_out = jnp.pad(out_weight.reshape(slice_rows, hw), ((0, 0), (0, 256 - hw)))
+    bias_parts = qv_bias.reshape(heads, 2, hd)
+    bias_qkv = order_columns(jnp.stack([bias_parts[:, 0], jnp.zeros_like(bias_parts[:, 0]), bias_parts[:, 1]], 1))
+    bias_qkv = jnp.pad(bias_qkv[None], ((0, 15), (0, 64)))
+    if grid.dp == 8 and grid.tensor == 4:
+        memory = memory_positions.shape[1]
+        place = jnp.pad(positions[None], ((0, 7), (0, 32 - memory)), constant_values=-1)
+        table = jnp.pad(memory_rows, ((0, 32 - memory), (0, 0)))
+        x0, x_all, q, k, v, w_qkv, up_g, down_g, out_g = entry(tokens, place, table, shard_qkv, bias_qkv, up_weight, down_weight, shard_out)
+        w_qkv = w_qkv.reshape(2, width, 9 * hd)
+        up_all = up_g.reshape(width, units)
+        ups = (up_all, grid.swap(up_all, 2))
+        downs = (down_g, grid.turn(down_g, 1, 1))
+        outs = (out_g, grid.turn(out_g, 1, 1))
+    else:
+        x0 = tokens.astype(f32) + jnp.dot(picks.astype(bf16), memory_rows, preferred_element_type=f32)
+        xl = x0.astype(bf16)
+        w_qkv = grid.gather(shard_qkv)
+        other = grid.swap(xl, 1)
+        x_all = jnp.concatenate([jnp.where(inner == 0, xl, other), jnp.where(inner == 0, other, xl)])
+        b_two = jnp.stack([bias_qkv[0], grid.swap(bias_qkv[0], 2)]).astype(f32)
+        y = [(mm(x_all, w_qkv[o]) + b_two[o, :9 * hd]).astype(bf16) for o in range(2)]
+        third = lambda n: [one[:, (6 + n) * hd:(7 + n) * hd] for one in y]
+        q, k, v = [jnp.concatenate([y[0][:, 2 * n * hd:2 * (n + 1) * hd], y[1][:, 2 * n * hd:2 * (n + 1) * hd]] + third(n), 1)
+                   for n in range(3)]
+        q = q * jnp.asarray(0.125, bf16)
+        outs, ups, downs = (grid.gather(shard_out, True),), (grid.gather(up_weight),), (grid.gather(down_weight, True),)
+    b_up = jnp.concatenate([up_bias, grid.swap(up_bias, 2)])
     b_up = jnp.stack([b_up, grid.swap(b_up, 1)]).astype(f32)
-    b_qkv = jnp.stack([qv[:, :, 0], jnp.zeros_like(qv[:, :, 0]), qv[:, :, 1]], 0).reshape(6 * hw)
-
-    joined = lambda w: w.transpose(1, 0, 2).reshape(width, -1)
-    w_out, w_up, w_down = joined(w_out), joined(w_up), joined(w_down)
-    w_out = (w_out, grid.swap(w_out, 1))
-    w_up = (w_up, grid.swap(w_up, 1))
-    w_down = (w_down, grid.swap(w_down, 1))
-
-    qkv = (jnp.dot(x_all, w_qkv, preferred_element_type=f32) + b_qkv).astype(bf16)
-    q = qkv[:, :2 * hw] * jnp.asarray(0.125, bf16)
-    k = qkv[:, 2 * hw:4 * hw]
-    v = qkv[:, 4 * hw:]
     mixed, lse = attend_forward(q, k, v, segments)
-    halves = mixed.reshape(2, rows, 2 * hw)
-    o_own = lax.dynamic_index_in_dim(halves, inner, 0, keepdims=False)
-    o_got = grid.swap(lax.dynamic_index_in_dim(halves, 1 - inner, 0, keepdims=False), 1)
-    o = (o_own, o_got)
-
-    attended = out_bias.astype(f32)
-    for side in range(2):
-        attended = attended + mm(o[side], w_out[side], NT)
-    r1 = x0 + attended
-    g1, s1 = norm1_gain.astype(f32), norm1_bias.astype(f32)
-    g2, s2 = norm2_gain.astype(f32), norm2_bias.astype(f32)
-    h1 = layer_norm(r1, g1, s1)
-    hl = h1.astype(bf16)
-    u = [mm(hl, w_up[side]) + b_up[side] for side in range(2)]
-    z = [gelu_exact(one).astype(bf16) for one in u]
-    r2 = h1 + down_bias.astype(f32)
-    for side in range(2):
-        r2 = r2 + mm(z[side], w_down[side], NT)
-    block_out = layer_norm(r2, g2, s2).astype(bf16)
-    cot = out_cotangent.astype(f32)
-    dr2, dg2, ds2 = jax.vjp(layer_norm, r2, g2, s2)[1](cot)
-    dfl = dr2.astype(bf16)
-    d_down_bias = jnp.sum(dfl.astype(f32), axis=0)
+    vec = jnp.stack([out_bias, norm1_gain, norm1_bias, down_bias, norm2_gain, norm2_bias, norm2_bias, norm2_bias]).astype(f32)
+    (block_out, dr1, do_all, g_down, g_up, g_out, sums, up_sums) = middle(
+        mixed, x0, outs, ups, downs, out_cotangent, vec, b_up.reshape(4, 1, units))
     TN = (((0,), (0,)), ((), ()))
-    g_down = [mm(dfl, z[side], TN) for side in range(2)]
-    dul = [jax.vjp(gelu_exact, u[side])[1](mm(dfl, w_down[side]))[0].astype(bf16) for side in range(2)]
-    g_up = [mm(hl, dul[side], TN) for side in range(2)]
-    d_up_bias = [jnp.sum(dul[side].astype(f32), axis=0) for side in range(2)]
-    dh1 = dr2
-    for side in range(2):
-        dh1 = dh1 + mm(dul[side], w_up[side], NT)
-    dr1, dg1, ds1 = jax.vjp(layer_norm, r1, g1, s1)[1](dh1)
-    dal = dr1.astype(bf16)
-    d_out_bias = jnp.sum(dal.astype(f32), axis=0)
-    g_out = [mm(dal, o[side], TN) for side in range(2)]
-    dol = [mm(dal, w_out[side]).astype(bf16) for side in range(2)]
-    got = grid.swap(dol[1], 1)
-    do_all = jnp.concatenate([jnp.where(inner == 0, dol[0], got), jnp.where(inner == 0, got, dol[0])])
-
-    def spread(pair, outer_first):
-        own = pair[0] + grid.swap(pair[1].astype(bf16), 1).astype(f32)
-        own = own.reshape(width, 2, -1).transpose(1, 0, 2)
-        return grid.reduce(own, outer_first)
-
-    grad_down = spread(g_down, True)
-    grad_up = spread(g_up, False)
-    grad_out = spread(g_out, True)
-
-    dq, dk, dv = attend_backward(q, k, v, do_all, lse, segments)
-    d_qkv = jnp.concatenate([dq, dk, dv], axis=-1)
-    g_qkv = mm(x_all, d_qkv, TN)
-    d_bias = jnp.sum(d_qkv.astype(f32), axis=0).reshape(3, 2, hw)
-    part = mm(d_qkv, w_qkv, NT).reshape(2, rows, width)
+
+    tie = lax.optimization_barrier
+    kinds = (True, False, True)
+    state = [grid.open(parts, kind) for parts, kind in zip((g_down, g_up, g_out), kinds)]
+    step = lambda n, state: [grid.stage(value, kind, n) for value, kind in zip(state, kinds)]
+    late = [(1, 0, 2)[n] for n in range(3)]
+    d = [None] * 3
+    state, d[1] = step(0, state), attend_backward(1, q, k, v, do_all, lse, segments)
+    state, d[1], q = tie((state, d[1], q))
+    g_one = mm(x_all, d[1], TN).astype(bf16)
+    state, d[0] = step(1, state), attend_backward(0, q, k, v, do_all, lse, segments)
+    state, d[0], q, g_one = tie((state, d[0], q, g_one))
+    g_zero = mm(x_all, d[0], TN)
+    first = g_zero + grid.swap(g_one, 2).astype(f32)
+    state, d[2] = step(2, state), attend_backward(2, q, k, v, do_all, lse, segments)
+    state, d[2], first = tie((state, d[2], first))
+    for n in range(3, grid.stages):
+        state = step(n, state)
+    grad_down, grad_up, grad_out = state
+    grad_out = grad_out[:, :hw]
+
+    g_two = mm(x_all, d[2], TN)
+    side = lambda m, o: jnp.concatenate([m[:, (2 * n + o) * hd:(2 * n + o + 1) * hd] for n in range(3)], 1)
+    second = side(g_two, 0) + grid.swap(side(g_two, 1).astype(bf16), 2).astype(f32)
+    both = jnp.concatenate([first, second], 1).reshape(*grid.factors, slice_rows, 9 * hd)
+    for j in reversed(range(len(grid.factors))):
+        both = grid.reduce_stage(both, j, j)
+    restore = lambda p: jnp.stack([jnp.concatenate([p[..., 2 * n * hd:2 * (n + 1) * hd].reshape(*p.shape[:-1], 2, hd),
+                                                    p[..., None, (6 + n) * hd:(7 + n) * hd]], -2) for n in range(3)], -2)
+    grad_qkv = restore(both).reshape(slice_rows, heads, 3 * hd)
+    third = jnp.concatenate([w_qkv[o][:, (6 + n) * hd:(7 + n) * hd] for n in range(3) for o in range(2)], 1)
+    part = (mm(d[0], w_qkv[0][:, :6 * hd], NT) + mm(d[1], w_qkv[1][:, :6 * hd], NT) + mm(d[2], third, NT)).reshape(2, rows, width)
     mine = lax.dynamic_index_in_dim(part, inner, 0, keepdims=False)
     theirs = lax.dynamic_index_in_dim(part, 1 - inner, 0, keepdims=False).astype(bf16)
     grad_tokens = mine + grid.swap(theirs, 1).astype(f32) + dr1
-    grad_qkv = grid.reduce(g_qkv.reshape(width, 3, 2, hw).transpose(2, 0, 1, 3).reshape(2, width, 3 * hw), True)
-    grad_qkv = grad_qkv.reshape(slice_rows, 3, heads, hd).transpose(0, 2, 1, 3).reshape(slice_rows, heads, 3 * hd)
+    d_sum = [jnp.sum(one.astype(f32), axis=0) for one in d]
+    d_bias = [jnp.concatenate([d_sum[o]] + [d_sum[2][(2 * n + o) * hd:(2 * n + o + 1) * hd] for n in range(3)]) for o in range(2)]
+    dg2, ds2, d_down_bias, dg1, ds1, d_out_bias = jnp.sum(sums, axis=1)
+    d_up_bias = jnp.sum(up_sums, axis=1).reshape(2, 2 * units)
     grad_memory = jnp.dot(picks.astype(f32).T, grad_tokens, precision=lax.Precision.HIGHEST)
 
     order = jnp.arange(4, dtype=jnp.int32) ^ tensor
-    up_parts = jnp.concatenate(d_up_bias).reshape(2, 2, units).transpose(0, 1, 2)
+    up_parts = d_up_bias.reshape(2, 2, units)
     up_parts = jnp.stack([up_parts[0, 0], up_parts[1, 0], up_parts[0, 1], up_parts[1, 1]])[order]
-    nothing = jnp.zeros_like(d_bias[0, 0])
-    take = lambda o_: jnp.stack([d_bias[0, o_].reshape(heads, hd), d_bias[2, o_].reshape(heads, hd)], 1).reshape(-1)
+    take = lambda o: restore(d_bias[o])[:, 0::2].reshape(-1)
     blank = jnp.zeros((2 * hw,), f32)
     qv_parts = jnp.stack([take(0), blank, take(1), blank])[order]
     pieces = [grad_memory.reshape(-1), d_out_bias, dg1, ds1, d_down_bias, dg2, ds2, up_parts.reshape(-1), qv_parts.reshape(-1)]

time: 548 us -> 495 us (0.903)
  Pallas kernels: 118 us -> 285 us
  matrix products: 124 us -> 20.2 us
  local copies, waits for them, and re-layouts: 105 us -> 56.9 us
  other arithmetic: 53.9 us -> 25.7 us
  waiting for transfers between devices: 70.6 us -> 49.3 us
  starting transfers between devices: 67.5 us -> 47.2 us
    pallas_call x1 -> x5, Pallas kernels: 76.4 us -> 244 us  [the longest x3 114 us: attend_backward(): pl.pallas_call(functools.partial(backward_kernel, 2 * g), out_shape=jax.S...]
    dot_general x20 -> x6, matrix products: 115 us -> 18.9 us  [mm(): return lax.dot_general(a, b, dims, preferred_element_type=jnp.float32)]
    unnamed x192 -> x121, local copies, waits for them, and re-layouts: 36 us -> 8.14 us
    ppermute x32 -> x18, waiting for transfers between devices: 47.5 us -> 21 us  [turn(): return lax.ppermute(value, AXES, pairs)]
    ppermute x32 -> x18, starting transfers between devices: 49.8 us -> 34.7 us  [turn(): return lax.ppermute(value, AXES, pairs)]
    another operation x21 -> x17, local copies, waits for them, and re-layouts: 14 us -> 1.26 us  [the longest x1 0.65 us: shards(): dg2, ds2, d_down_bias, dg1, ds1, d_out_bias = jnp.sum(sums, axis=1)]
    ppermute x22 -> x11, waiting for transfers between devices: 7.71 us -> 19.5 us  [swap(): return lax.ppermute(value, AXES, pairs)]
    another operation x13 -> x8, other arithmetic: 10.2 us -> 0.09 us  [shards(): jnp.stack([jnp.concatenate([p[..., 2 * n * hd:2 * (n + 1) * hd].reshape(*...]
  transfers between devices with their start and end apart: 57 -> 32, of which waited for: 15 -> 13; matrix products, arithmetic and copies ran while one was open for 40% -> 11% of each run, Pallas kernels for 22% -> 24%
where the time goes in v2:
time: 495 us; the launch traced here: 487 us
  Pallas kernels  285 us (58%)
  local copies, waits for them, and re-layouts  56.9 us (11%)
  waiting for transfers between devices  49.3 us (10%)
  starting transfers between devices  47.2 us (10%)
  other arithmetic  25.7 us (5%)
  matrix products  20.2 us (4%)
    pallas_call x3, Pallas kernels, attend_backward(): pl.pallas_call(functools.partial(backward_kernel, 2 * g), out_shape=jax.S...  114 us
    pallas_call x1, Pallas kernels, middle(): pl.pallas_call(kernel, out_shape=(shape((rows, width), bf16), shape((rows...  73.8 us
    pallas_call x1, Pallas kernels, entry(): pl.pallas_call(entry_kernel, out_shape=(shape((rows, width), f32), shape(...  55.5 us
    pallas_call x1, Pallas kernels, attend_forward(): pl.pallas_call(forward_kernel, out_shape=(jax.ShapeDtypeStruct((n, width)...  41.5 us
    ppermute x18, starting transfers between devices, turn(): return lax.ppermute(value, AXES, pairs)  34.7 us
    ppermute x18, waiting for transfers between devices, turn(): return lax.ppermute(value, AXES, pairs)  21 us
    ppermute x11, waiting for transfers between devices, swap(): return lax.ppermute(value, AXES, pairs)  19.5 us
    dot_general x6, matrix products, mm(): return lax.dot_general(a, b, dims, preferred_element_type=jnp.float32)  18.9 us
  transfers between devices with their start and end apart: 32, of which 13 were waited for; matrix products, arithmetic and copies ran while one was open for 11% of the time, Pallas kernels for 24%

profile of v2, /device:TPU:0, one launch (start us, length us, event | category | flops | bytes accessed | tf_op | source)
XLA Modules:
  0.0 486.7 jit_solution(8167457792279465777)
XLA Ops:
  9.1 55.5 %entry.1 = (f32[1024,768]{1,0:T(8,128)}, bf16[2048,768]{1,0:T(8,128)(2,1)}, bf16[2048,384]{1,0:T(8,128)(2,1)}, bf16[2048,384]{1,0:T(8,128)(2,1)}, bf16[2048,384]...) custom-call(bf16[1024,768]{1,0:T(8,128)(2,1)} %tokens.1, ...), custom_call_target="tpu_custom_call" | custom-call | flops 3623878656 | bytes 20000000 | tf_op jit(solution)/shard_map/entry/pallas_call | solution.py:706
  68.7 1.7 fusion.37
  75.8 41.5 %attend_forward.1 = (bf16[2048,384]{1,0:T(8,128)(2,1)}, f32[8,2048]{1,0:T(8,128)}) custom-call(s32[8]{0:T(128)} %slice.306.first_ref, s32[8]{0:T(128)} %slice.307.last_ref, bf16[2048,384]{1,0:T(8,128)(2,1)} %get-tuple-element.75.q_ref, bf16[2048,384]{1,0:T(8,128)(2,1)} %get-tuple-element.51.k_ref, bf16[2048,384]{1,0:T(8,128)(2,1)} %get-tuple-element.52.v_ref, ...), custom_call_target="tpu_custom_call" | custom-call | flops 6442450944 | bytes 6291456 | tf_op jit(solution)/shard_map/attend_forward/pallas_call | solution.py:105
  119.7 2.2 concatenate.55
  122.7 73.8 %middle.1 = (bf16[1024,768]{1,0:T(8,128)(2,1)}, f32[1024,768]{1,0:T(8,128)}, bf16[2048,384]{1,0:T(8,128)(2,1)}, bf16[2,768,768]{2,1,0:T(8,128)(2,1)}, bf16[2,768...) custom-call(bf16[2048,384]{1,0:T(8,128)(2,1)} %get-tuple-element.53.o_all, ...), custom_call_target="tpu_custom_call" | custom-call | flops 32614907904 | bytes 60000000 | tf_op jit(solution)/shard_map/middle/pallas_call | solution.py:540
  196.5 1.9 slice_bitcast_fusion.1
  198.4 2.4 dynamic-slice_bitcast_fusion
  200.8 2.0 collective-permute-start.6
  203.9 1.5 collective-permute-start.5
  207.4 38.2 %attend_backward.3 = bf16[2048,384]{1,0:T(8,128)(2,1)} custom-call(s32[8]{0:T(128)} %slice.306.first_ref, s32[8]{0:T(128)} %slice.307.last_ref, bf16[2048,384]{1,0:T(8,128)(2,1)} %get-tuple-element.75.q_ref, bf16[2048,384]{1,0:T(8,128)(2,1)} %get-tuple-element.62.do_ref, bf16[2048,384]{1,0:T(8,128)(2,1)} %get-tuple-element.51.k_ref, ...), custom_call_target="tpu_custom_call" | custom-call | flops 5368709120 | bytes 3670016 | tf_op jit(solution)/shard_map/attend_backward/pallas_call | solution.py:219
  245.6 2.2 convert_add_fusion.3
  247.8 3.5 convert_add_fusion.1
  251.3 3.1 convert_add_fusion
  254.4 4.5 fusion.4
  258.8 2.6 convolution_convert_fusion
  261.5 38.3 %attend_backward.4 = bf16[2048,384]{1,0:T(8,128)(2,1)} custom-call(s32[8]{0:T(128)} %slice.306.first_ref, s32[8]{0:T(128)} %slice.307.last_ref, bf16[2048,384]{1,0:T(8,128)(2,1)} %get-tuple-element.75.q_ref, bf16[2048,384]{1,0:T(8,128)(2,1)} %get-tuple-element.62.do_ref, bf16[2048,384]{1,0:T(8,128)(2,1)} %get-tuple-element.51.k_ref, ...), custom_call_target="tpu_custom_call" | custom-call | flops 5368709120 | bytes 3670016 | tf_op jit(solution)/shard_map/attend_backward/pallas_call | solution.py:219
  301.5 2.2 fusion.3
  303.7 2.2 fusion.2
  310.4 8.0 %collective-permute-done.9 = bf16[4,96,768]{2,1,0:T(8,128)(2,1)} collective-permute-done((bf16[4,96,768]{2,1,0:T(8,128)(2,1)}, bf16[4,96,768]{2,1,0:T(8,128)(2,1)}, u32[]{:S(2)}, u32[]{:S(2)}) %collective-permute-start.9) | collective-permute-done | bytes 589856 | tf_op jit(solution)/shard_map/ppermute | solution.py:774
  318.5 2.2 bitcast_add_fusion.2
  320.7 2.4 bitcast_add_fusion.3
  323.4 4.5 fusion.6
  329.5 38.0 %attend_backward.5 = bf16[2048,384]{1,0:T(8,128)(2,1)} custom-call(s32[8]{0:T(128)} %slice.306.first_ref, s32[8]{0:T(128)} %slice.307.last_ref, bf16[2048,384]{1,0:T(8,128)(2,1)} %get-tuple-element.75.q_ref, bf16[2048,384]{1,0:T(8,128)(2,1)} %get-tuple-element.62.do_ref, bf16[2048,384]{1,0:T(8,128)(2,1)} %get-tuple-element.51.k_ref, ...), custom_call_target="tpu_custom_call" | custom-call | flops 5368709120 | bytes 3670016 | tf_op jit(solution)/shard_map/attend_backward/pallas_call | solution.py:219
  368.6 6.3 %collective-permute-start.18 = (bf16[96,256]{1,0:T(8,128)(2,1)S(1)}, bf16[96,256]{1,0:T(8,128)(2,1)}, u32[]{:S(2)}, u32[]{:S(2)}) collective-permute-start(bf16[96,256]{1,0:T(8,128)(2,1)S(1)} %get-tuple-element.148), channel_id=1, source_target_pairs={{0,16},{1,17},{2,18},{3,19},{4,20},{5,21},{6,22},{7,23},{8,24},{9,... | collective-permute-start | bytes 147464 | tf_op jit(solution)/shard_map/ppermute | solution.py:766
  374.9 2.8 collective-permute-start.19
  377.7 1.9 fusion.23
  379.7 2.1 fusion.20
  384.9 3.3 collective-permute-start.16
  391.3 6.5 %collective-permute-done.15 = bf16[96,768]{1,0:T(8,128)(2,1)S(1)} collective-permute-done((bf16[96,768]{1,0:T(8,128)(2,1)}, bf16[96,768]{1,0:T(8,128)(2,1)S(1)}, u32[]{:S(2)}, u32[]{:S(2)}) %collective-permute-start.15) | collective-permute-done | bytes 147488 | tf_op jit(solution)/shard_map/ppermute | solution.py:766
  397.8 5.2 %collective-permute-start.13 = (bf16[96,768]{1,0:T(8,128)(2,1)}, bf16[96,768]{1,0:T(8,128)(2,1)S(1)}, u32[]{:S(2)}, u32[]{:S(2)}) collective-permute-start(bf16[96,768]{1,0:T(8,128)(2,1)} %get-tuple-element.135), channel_id=1, source_target_pairs={{0,24},{1,25},{2,26},{3,27},{4,28},{5,29},{6,30},{7,31},{8,0},{9,1... | collective-permute-start | bytes 442376 | tf_op jit(solution)/shard_map/ppermute | solution.py:766
  403.0 1.7 fusion.14
  404.7 1.8 collective-permute-done.12
  406.5 1.9 fusion.16
  408.5 3.6 convert_add_fusion.2
  412.1 1.8 fusion.48
  415.1 1.9 add_add_fusion
  418.7 5.9 %collective-permute-done.27 = bf16[768,192]{1,0:T(8,128)(2,1)S(1)} collective-permute-done((bf16[768,192]{1,0:T(8,128)(2,1)S(1)}, bf16[768,192]{1,0:T(8,128)(2,1)S(1)}, u32[]{:S(2)}, u32[]{:S(2)}) %collective-permute-start.27) | collective-permute-done | bytes 294944 | tf_op jit(solution)/shard_map/ppermute | solution.py:774
  428.3 8.0 %collective-permute-done.28 = bf16[4,96,576]{2,1,0:T(8,128)(2,1)} collective-permute-done((bf16[4,96,576]{2,1,0:T(8,128)(2,1)S(1)}, bf16[4,96,576]{2,1,0:T(8,128)(2,1)}, u32[]{:S(2)}, u32[]{:S(2)}) %collective-permute-start.28) | collective-permute-done | bytes 442400 | tf_op jit(solution)/shard_map/ppermute | solution.py:766
  437.8 4.5 collective-permute-start.29
  442.3 2.4 collective-permute-start.31
  446.8 4.5 collective-permute-done.30
  451.4 3.8 fusion
  461.9 4.3 collective-permute-done.23
  467.5 3.5 collective-permute-done.24
  470.9 3.4 collective-permute-start.25
  474.4 2.6 collective-permute-done.25
  477.0 1.9 collective-permute-start.26
  479.8 2.7 collective-permute-done.26
  (289 shorter events, 61.8 us)
Async XLA Ops:
  0.6 68.1 %copy-start = (s32[2,2048]{1,0:T(2,128)S(1)}, s32[2,2048]{1,0:T(2,128)}, u32[]{:S(2)}) copy-start(s32[2,2048]{1,0:T(2,128)} %param.18) | copy-start | bytes 49156
  9.1 58.1 %copy-start.40 = (bf16[768]{0:T(1024)(128)(2,1)S(1)}, bf16[768]{0:T(1024)(128)(2,1)}, u32[]{:S(2)}) copy-start(bf16[768]{0:T(1024)(128)(2,1)} %param.28) | copy-start | bytes 4612
  64.6 58.1 %collective-permute-start.1 = (bf16[768,768]{1,0:T(8,128)(2,1)}, bf16[768,768]{1,0:T(8,128)(2,1)}, u32[]{:S(2)}, u32[]{:S(2)}) collective-permute-start(bf16[768,768]{1,0:T(8,128)(2,1)} %bitcast.216), channel_id=1, source_target_pairs={{0,2},{1,3},{2,0},{3,1},{4,6},{5,7},{6,4},{7,5},{8,10},{9,11},{10,... | collective-permute-start | bytes 3538952 | tf_op jit(solution)/shard_map/ppermute | solution.py:774
  65.1 57.5 %collective-permute-start.2 = (bf16[2,4,96,768]{3,2,1,0:T(8,128)(2,1)}, bf16[2,4,96,768]{3,2,1,0:T(8,128)(2,1)}, u32[]{:S(2)}, u32[]{:S(2)}) collective-permute-start(bf16[2,4,96,768]{3,2,1,0:T(8,128)(2,1)} %get-tuple-element.57.refs_4_), channel_id=1, source_target_pairs={{0,4},{1,5},{2,6},{3,7},{4,0},{5,1},{6,2},{7,3},{8,12},{9,13},{10,... | collective-permute-start | bytes 3538952 | tf_op jit(solution)/shard_map/ppermute | solution.py:766
  66.6 56.0 %collective-permute-start = (bf16[2,4,96,256]{3,2,1,0:T(8,128)(2,1)}, bf16[2,4,96,256]{3,2,1,0:T(8,128)(2,1)}, u32[]{:S(2)}, u32[]{:S(2)}) collective-permute-start(bf16[2,4,96,256]{3,2,1,0:T(8,128)(2,1)} %get-tuple-element.55.refs_0_), channel_id=1, source_target_pairs={{0,4},{1,5},{2,6},{3,7},{4,0},{5,1},{6,2},{7,3},{8,12},{9,13},{10,... | collective-permute-start | bytes 1179656 | tf_op jit(solution)/shard_map/ppermute | solution.py:766
  67.2 51.5 %collective-permute-start.3 = (bf16[768]{0:T(1024)(128)(2,1)S(1)}, bf16[768]{0:T(1024)(128)(2,1)S(1)}, u32[]{:S(2)}, u32[]{:S(2)}) collective-permute-start(bf16[768]{0:T(1024)(128)(2,1)S(1)} %copy-done.40), channel_id=1, source_target_pairs={{0,2},{1,3},{2,0},{3,1},{4,6},{5,7},{6,4},{7,5},{8,10},{9,11},{10,... | collective-permute-start | bytes 4616 | tf_op jit(solution)/shard_map/ppermute | solution.py:774
  73.8 131.7 %copy-start.31 = (s32[1024]{0:T(1024)}, s32[1024]{0:T(1024)S(1)}, u32[]{:S(2)}) copy-start(s32[1024]{0:T(1024)S(1)} %pad_clamp_fusion) | copy-start | bytes 12292
  75.8 41.5 %copy-start.48 = (s32[2,20]{1,0:T(2,128)S(1)}, s32[2,20]{1,0:T(2,128)}, u32[]{:S(2)}) copy-start(s32[2,20]{1,0:T(2,128)} %param.19) | copy-start | bytes 484
  75.8 43.2 %copy-start.34 = (bf16[768]{0:T(1024)(128)(2,1)S(1)}, bf16[768]{0:T(1024)(128)(2,1)}, u32[]{:S(2)}) copy-start(bf16[768]{0:T(1024)(128)(2,1)} %param.24) | copy-start | bytes 4612
  75.8 43.2 %copy-start.35 = (bf16[768]{0:T(1024)(128)(2,1)S(1)}, bf16[768]{0:T(1024)(128)(2,1)}, u32[]{:S(2)}) copy-start(bf16[768]{0:T(1024)(128)(2,1)} %param.25) | copy-start | bytes 4612
  75.8 43.2 %copy-start.36 = (bf16[768]{0:T(1024)(128)(2,1)S(1)}, bf16[768]{0:T(1024)(128)(2,1)}, u32[]{:S(2)}) copy-start(bf16[768]{0:T(1024)(128)(2,1)} %param.26) | copy-start | bytes 4612
  75.8 43.2 %copy-start.37 = (bf16[768]{0:T(1024)(128)(2,1)S(1)}, bf16[768]{0:T(1024)(128)(2,1)}, u32[]{:S(2)}) copy-start(bf16[768]{0:T(1024)(128)(2,1)} %param.30) | copy-start | bytes 4612
  75.8 43.2 %copy-start.38 = (bf16[768]{0:T(1024)(128)(2,1)S(1)}, bf16[768]{0:T(1024)(128)(2,1)}, u32[]{:S(2)}) copy-start(bf16[768]{0:T(1024)(128)(2,1)} %param.31) | copy-start | bytes 4612
  75.8 43.2 %copy-start.39 = (bf16[768]{0:T(1024)(128)(2,1)S(1)}, bf16[768]{0:T(1024)(128)(2,1)}, u32[]{:S(2)}) copy-start(bf16[768]{0:T(1024)(128)(2,1)} %param.32) | copy-start | bytes 4612
  118.8 3.1 collective-permute-start.4
  198.4 47.2 %collective-permute-start.7 = (bf16[768,256]{1,0:T(8,128)(2,1)}, bf16[768,256]{1,0:T(8,128)(2,1)}, u32[]{:S(2)}, u32[]{:S(2)}) collective-permute-start(bf16[768,256]{1,0:T(8,128)(2,1)} %slice_bitcast_fusion.1), channel_id=1, source_target_pairs={{0,2},{1,3},{2,0},{3,1},{4,6},{5,7},{6,4},{7,5},{8,10},{9,11},{10,... | collective-permute-start | bytes 1179656 | tf_op jit(solution)/shard_map/ppermute | solution.py:774
  200.8 50.5 %collective-permute-start.6 = (bf16[2,4,96,768]{3,2,1,0:T(8,128)(2,1)}, bf16[2,4,96,768]{3,2,1,0:T(8,128)(2,1)}, u32[]{:S(2)}, u32[]{:S(2)}) collective-permute-start(bf16[2,4,96,768]{3,2,1,0:T(8,128)(2,1)} %dynamic-slice_bitcast_fusion), channel_id=1, source_target_pairs={{0,4},{1,5},{2,6},{3,7},{4,0},{5,1},{6,2},{7,3},{8,12},{9,13},{10,... | collective-permute-start | bytes 3538952 | tf_op jit(solution)/shard_map/ppermute | solution.py:766
  203.9 43.9 %collective-permute-start.5 = (bf16[768,768]{1,0:T(8,128)(2,1)}, bf16[768,768]{1,0:T(8,128)(2,1)}, u32[]{:S(2)}, u32[]{:S(2)}) collective-permute-start(bf16[768,768]{1,0:T(8,128)(2,1)} %slice_bitcast_fusion), channel_id=1, source_target_pairs={{0,2},{1,3},{2,0},{3,1},{4,6},{5,7},{6,4},{7,5},{8,10},{9,11},{10,... | collective-permute-start | bytes 3538952 | tf_op jit(solution)/shard_map/ppermute | solution.py:774
  300.9 8.7 %collective-permute-start.10 = (bf16[4,96,256]{2,1,0:T(8,128)(2,1)S(1)}, bf16[4,96,256]{2,1,0:T(8,128)(2,1)S(1)}, u32[]{:S(2)}, u32[]{:S(2)}) collective-permute-start(bf16[4,96,256]{2,1,0:T(8,128)(2,1)S(1)} %fusion.19), channel_id=1, source_target_pairs={{0,4},{1,5},{2,6},{3,7},{4,0},{5,1},{6,2},{7,3},{8,12},{9,13},{10,... | collective-permute-start | bytes 589832 | tf_op jit(solution)/shard_map/ppermute | solution.py:766
  303.7 14.8 %collective-permute-start.9 = (bf16[4,96,768]{2,1,0:T(8,128)(2,1)}, bf16[4,96,768]{2,1,0:T(8,128)(2,1)}, u32[]{:S(2)}, u32[]{:S(2)}) collective-permute-start(bf16[4,96,768]{2,1,0:T(8,128)(2,1)} %fusion.3), channel_id=1, source_target_pairs={{0,2},{1,3},{2,0},{3,1},{4,6},{5,7},{6,4},{7,5},{8,10},{9,11},{10,... | collective-permute-start | bytes 1769480 | tf_op jit(solution)/shard_map/ppermute | solution.py:774
  305.9 12.5 %copy-start.11 = (f32[2,4,96,768]{3,2,1,0:T(8,128)S(1)}, f32[2,4,96,768]{3,2,1,0:T(8,128)}, u32[]{:S(2)}) copy-start(f32[2,4,96,768]{3,2,1,0:T(8,128)} %convert_add_fusion) | copy-start | bytes 7077892
  305.9 14.8 %collective-permute-start.8 = (bf16[4,96,768]{2,1,0:T(8,128)(2,1)}, bf16[4,96,768]{2,1,0:T(8,128)(2,1)}, u32[]{:S(2)}, u32[]{:S(2)}) collective-permute-start(bf16[4,96,768]{2,1,0:T(8,128)(2,1)} %fusion.2), channel_id=1, source_target_pairs={{0,4},{1,5},{2,6},{3,7},{4,0},{5,1},{6,2},{7,3},{8,12},{9,13},{10,... | collective-permute-start | bytes 1769480 | tf_op jit(solution)/shard_map/ppermute | solution.py:766
  310.4 10.3 %copy-start.10 = (f32[768,768]{1,0:T(8,128)S(1)}, f32[768,768]{1,0:T(8,128)}, u32[]{:S(2)}) copy-start(f32[768,768]{1,0:T(8,128)} %convert_add_fusion.1) | copy-start | bytes 7077892
  328.0 80.5 %collective-permute-start.20 = (bf16[768,384]{1,0:T(8,128)(2,1)}, bf16[768,384]{1,0:T(8,128)(2,1)}, u32[]{:S(2)}, u32[]{:S(2)}) collective-permute-start(bf16[768,384]{1,0:T(8,128)(2,1)} %convolution_convert_fusion), channel_id=1, source_target_pairs={{0,2},{1,3},{2,0},{3,1},{4,6},{5,7},{6,4},{7,5},{8,10},{9,11},{10,... | collective-permute-start | bytes 1769480 | tf_op jit(solution)/shard_map/ppermute | solution.py:774
  368.5 15.2 %collective-permute-start.17 = (bf16[96,256]{1,0:T(8,128)(2,1)S(1)}, bf16[96,256]{1,0:T(8,128)(2,1)S(1)}, u32[]{:S(2)}, u32[]{:S(2)}) collective-permute-start(bf16[96,256]{1,0:T(8,128)(2,1)S(1)} %get-tuple-element.146), channel_id=1, source_target_pairs={{0,8},{1,9},{2,10},{3,11},{4,12},{5,13},{6,14},{7,15},{8,16},{9,17... | collective-permute-start | bytes 147464 | tf_op jit(solution)/shard_map/ppermute | solution.py:766
  368.6 16.3 %collective-permute-start.18 = (bf16[96,256]{1,0:T(8,128)(2,1)S(1)}, bf16[96,256]{1,0:T(8,128)(2,1)}, u32[]{:S(2)}, u32[]{:S(2)}) collective-permute-start(bf16[96,256]{1,0:T(8,128)(2,1)S(1)} %get-tuple-element.148), channel_id=1, source_target_pairs={{0,16},{1,17},{2,18},{3,19},{4,20},{5,21},{6,22},{7,23},{8,24},{9,... | collective-permute-start | bytes 147464 | tf_op jit(solution)/shard_map/ppermute | solution.py:766
  374.9 13.3 %collective-permute-start.19 = (bf16[96,256]{1,0:T(8,128)(2,1)S(1)}, bf16[96,256]{1,0:T(8,128)(2,1)}, u32[]{:S(2)}, u32[]{:S(2)}) collective-permute-start(bf16[96,256]{1,0:T(8,128)(2,1)S(1)} %get-tuple-element.147), channel_id=1, source_target_pairs={{0,24},{1,25},{2,26},{3,27},{4,28},{5,29},{6,30},{7,31},{8,0},{9,1... | collective-permute-start | bytes 147464 | tf_op jit(solution)/shard_map/ppermute | solution.py:766
  379.7 10.1 %collective-permute-start.14 = (bf16[96,768]{1,0:T(8,128)(2,1)}, bf16[96,768]{1,0:T(8,128)(2,1)S(1)}, u32[]{:S(2)}, u32[]{:S(2)}) collective-permute-start(bf16[96,768]{1,0:T(8,128)(2,1)} %get-tuple-element.131), channel_id=1, source_target_pairs={{0,8},{1,9},{2,10},{3,11},{4,12},{5,13},{6,14},{7,15},{8,16},{9,17... | collective-permute-start | bytes 442376 | tf_op jit(solution)/shard_map/ppermute | solution.py:766
  379.7 28.8 %copy-start.3 = (bf16[2048,768]{1,0:T(8,128)(2,1)S(1)}, bf16[2048,768]{1,0:T(8,128)(2,1)}, u32[]{:S(2)}) copy-start(bf16[2048,768]{1,0:T(8,128)(2,1)} %get-tuple-element.68) | copy-start | bytes 9437188
  384.4 13.4 %collective-permute-start.15 = (bf16[96,768]{1,0:T(8,128)(2,1)}, bf16[96,768]{1,0:T(8,128)(2,1)S(1)}, u32[]{:S(2)}, u32[]{:S(2)}) collective-permute-start(bf16[96,768]{1,0:T(8,128)(2,1)} %get-tuple-element.133), channel_id=1, source_target_pairs={{0,16},{1,17},{2,18},{3,19},{4,20},{5,21},{6,22},{7,23},{8,24},{9,... | collective-permute-start | bytes 442376 | tf_op jit(solution)/shard_map/ppermute | solution.py:766
  384.9 18.1 %collective-permute-start.16 = (bf16[96,768]{1,0:T(8,128)(2,1)}, bf16[96,768]{1,0:T(8,128)(2,1)S(1)}, u32[]{:S(2)}, u32[]{:S(2)}) collective-permute-start(bf16[96,768]{1,0:T(8,128)(2,1)} %get-tuple-element.132), channel_id=1, source_target_pairs={{0,24},{1,25},{2,26},{3,27},{4,28},{5,29},{6,30},{7,31},{8,0},{9,1... | collective-permute-start | bytes 442376 | tf_op jit(solution)/shard_map/ppermute | solution.py:766
  388.2 16.5 %collective-permute-start.11 = (bf16[96,768]{1,0:T(8,128)(2,1)}, bf16[96,768]{1,0:T(8,128)(2,1)S(1)}, u32[]{:S(2)}, u32[]{:S(2)}) collective-permute-start(bf16[96,768]{1,0:T(8,128)(2,1)} %get-tuple-element.134), channel_id=1, source_target_pairs={{0,8},{1,9},{2,10},{3,11},{4,12},{5,13},{6,14},{7,15},{8,16},{9,17... | collective-permute-start | bytes 442376 | tf_op jit(solution)/shard_map/ppermute | solution.py:766
  389.8 16.7 %collective-permute-start.12 = (bf16[96,768]{1,0:T(8,128)(2,1)}, bf16[96,768]{1,0:T(8,128)(2,1)S(1)}, u32[]{:S(2)}, u32[]{:S(2)}) collective-permute-start(bf16[96,768]{1,0:T(8,128)(2,1)} %get-tuple-element.136), channel_id=1, source_target_pairs={{0,16},{1,17},{2,18},{3,19},{4,20},{5,21},{6,22},{7,23},{8,24},{9,... | collective-permute-start | bytes 442376 | tf_op jit(solution)/shard_map/ppermute | solution.py:766
  397.8 8.7 %collective-permute-start.13 = (bf16[96,768]{1,0:T(8,128)(2,1)}, bf16[96,768]{1,0:T(8,128)(2,1)S(1)}, u32[]{:S(2)}, u32[]{:S(2)}) collective-permute-start(bf16[96,768]{1,0:T(8,128)(2,1)} %get-tuple-element.135), channel_id=1, source_target_pairs={{0,24},{1,25},{2,26},{3,27},{4,28},{5,29},{6,30},{7,31},{8,0},{9,1... | collective-permute-start | bytes 442376 | tf_op jit(solution)/shard_map/ppermute | solution.py:766
  406.5 8.3 %slice-start.2 = ((s8[6291456]{0:T(1024)(128)(4,1)}), s8[4194304]{0:T(1024)(128)(4,1)S(1)}, s32[]{:S(2)}) async-start(s8[6291456]{0:T(1024)(128)(4,1)} %bitcast.181), calls=%async_computation.2 | async-start | bytes 8388608
  414.6 9.9 %collective-permute-start.27 = (bf16[768,192]{1,0:T(8,128)(2,1)S(1)}, bf16[768,192]{1,0:T(8,128)(2,1)S(1)}, u32[]{:S(2)}, u32[]{:S(2)}) collective-permute-start(bf16[768,192]{1,0:T(8,128)(2,1)S(1)} %pad_maximum_fusion.1), channel_id=1, source_target_pairs={{0,2},{1,3},{2,0},{3,1},{4,6},{5,7},{6,4},{7,5},{8,10},{9,11},{10,... | collective-permute-start | bytes 884744 | tf_op jit(solution)/shard_map/ppermute | solution.py:774
  416.9 8.1 %copy-start.4 = (f32[2048,768]{1,0:T(8,128)}, f32[2048,768]{1,0:T(8,128)S(1)}, u32[]{:S(2)}) copy-start(f32[2048,768]{1,0:T(8,128)S(1)} %add_add_fusion) | copy-start | bytes 18874372
  418.5 32.9 %collective-permute-start.21 = (bf16[1024,768]{1,0:T(8,128)(2,1)}, bf16[1024,768]{1,0:T(8,128)(2,1)}, u32[]{:S(2)}, u32[]{:S(2)}) collective-permute-start(bf16[1024,768]{1,0:T(8,128)(2,1)} %fusion.1), channel_id=1, source_target_pairs={{0,1},{1,0},{2,3},{3,2},{4,5},{5,4},{6,7},{7,6},{8,9},{9,8},{10,11... | collective-permute-start | bytes 4718600 | tf_op jit(solution)/shard_map/ppermute | solution.py:774
  425.0 11.2 %collective-permute-start.28 = (bf16[4,96,576]{2,1,0:T(8,128)(2,1)S(1)}, bf16[4,96,576]{2,1,0:T(8,128)(2,1)}, u32[]{:S(2)}, u32[]{:S(2)}) collective-permute-start(bf16[4,96,576]{2,1,0:T(8,128)(2,1)S(1)} %fusion.10), channel_id=1, source_target_pairs={{0,4},{1,5},{2,6},{3,7},{4,0},{5,1},{6,2},{7,3},{8,12},{9,13},{10,... | collective-permute-start | bytes 1327112 | tf_op jit(solution)/shard_map/ppermute | solution.py:766
  437.8 9.0 %collective-permute-start.29 = (bf16[96,576]{0,1:T(8,128)(2,1)S(1)}, bf16[96,576]{0,1:T(8,128)(2,1)S(1)}, u32[]{:S(2)}, u32[]{:S(2)}) collective-permute-start(bf16[96,576]{0,1:T(8,128)(2,1)S(1)} %get-tuple-element.125), channel_id=1, source_target_pairs={{0,8},{1,9},{2,10},{3,11},{4,12},{5,13},{6,14},{7,15},{8,16},{9,17... | collective-permute-start | bytes 331784 | tf_op jit(solution)/shard_map/ppermute | solution.py:766
  442.3 9.0 %collective-permute-start.30 = (bf16[96,576]{0,1:T(8,128)(2,1)S(1)}, bf16[96,576]{0,1:T(8,128)(2,1)S(1)}, u32[]{:S(2)}, u32[]{:S(2)}) collective-permute-start(bf16[96,576]{0,1:T(8,128)(2,1)S(1)} %get-tuple-element.127), channel_id=1, source_target_pairs={{0,16},{1,17},{2,18},{3,19},{4,20},{5,21},{6,22},{7,23},{8,24},{9,... | collective-permute-start | bytes 331784 | tf_op jit(solution)/shard_map/ppermute | solution.py:766
  442.3 9.0 %collective-permute-start.31 = (bf16[96,576]{0,1:T(8,128)(2,1)S(1)}, bf16[96,576]{0,1:T(8,128)(2,1)S(1)}, u32[]{:S(2)}, u32[]{:S(2)}) collective-permute-start(bf16[96,576]{0,1:T(8,128)(2,1)S(1)} %get-tuple-element.126), channel_id=1, source_target_pairs={{0,24},{1,25},{2,26},{3,27},{4,28},{5,29},{6,30},{7,31},{8,0},{9,1... | collective-permute-start | bytes 331784 | tf_op jit(solution)/shard_map/ppermute | solution.py:766
  459.9 1.4 collective-permute-start.22
  461.3 4.9 %collective-permute-start.23 = (f32[24576]{0:T(1024)S(1)}, f32[24576]{0:T(1024)S(1)}, u32[]{:S(2)}, u32[]{:S(2)}) collective-permute-start(f32[24576]{0:T(1024)S(1)} %add.292), channel_id=1, source_target_pairs={{0,2},{1,3},{2,0},{3,1},{4,6},{5,7},{6,4},{7,5},{8,10},{9,11},{10,... | collective-permute-start | bytes 294920 | tf_op jit(solution)/shard_map/ppermute | solution.py:774
  466.2 4.7 collective-permute-start.24
  467.4 17.6 %copy-start.20 = (bf16[1024,768]{1,0:T(8,128)(2,1)S(1)}, bf16[1024,768]{1,0:T(8,128)(2,1)}, u32[]{:S(2)}) copy-start(bf16[1024,768]{1,0:T(8,128)(2,1)} %get-tuple-element.213) | copy-start | bytes 4718596
  470.9 6.0 %collective-permute-start.25 = (f32[24576]{0:T(1024)S(1)}, f32[24576]{0:T(1024)S(1)}, u32[]{:S(2)}, u32[]{:S(2)}) collective-permute-start(f32[24576]{0:T(1024)S(1)} %add.294), channel_id=1, source_target_pairs={{0,8},{1,9},{2,10},{3,11},{4,12},{5,13},{6,14},{7,15},{8,0},{9,1},... | collective-permute-start | bytes 294920 | tf_op jit(solution)/shard_map/ppermute | solution.py:770
  477.0 5.6 %collective-permute-start.26 = (f32[24576]{0:T(1024)S(1)}, f32[24576]{0:T(1024)S(1)}, u32[]{:S(2)}, u32[]{:S(2)}) collective-permute-start(f32[24576]{0:T(1024)S(1)} %add.295), channel_id=1, source_target_pairs={{0,16},{1,17},{2,18},{3,19},{4,20},{5,21},{6,22},{7,23},{8,24},{9,... | collective-permute-start | bytes 294920 | tf_op jit(solution)/shard_map/ppermute | solution.py:770
  (37 other events, 133.2 us)
